TPU v7x, 128 devices: a whole 4x4x4 slice. The times are simulated.
128 devices in a mesh: rad: 4 (over y), lon: 32 (over x, z, core).
Axes of the slice: x: 4, y: 4, z: 4, core: 2. Of those that a mesh axis runs over, the one named last changes fastest.
Arguments:
- state: float32 [8, 256, 512, 256], P(None, 'rad', 'lon'), may hold values from -6 to 6
- flux_matrices: float32 [2, 8, 8], replicated, may hold values from -2 to 2
- wave_speed: float32 [2], replicated, may hold values from 0.5 to 2
- flux_volume: float32 [256, 512, 256], P('rad', 'lon'), may hold values from 0.02 to 0.2
- block_tile: int32 [32, 256, 1], P('lon', 'rad'), may hold values from 0 to 127; in each aligned block of 64 rows (0 to 63, 64 to 127, ..., all dimensions but the last counted through in order) at most 2 rows name the same one
- tile_of_device: int32 [128], replicated, may hold values from 0 to 127, each once
- phase_density: float32 [128, 200, 128], P(('rad', 'lon')), may hold values from -6 to 6
- injection: float32 [2, 200], replicated, may hold values from -3 to 3
- drift_courant: float32 [200], replicated, may hold values from 0.05 to 0.9
- energy_weight: float32 [200], replicated, may hold values from 0.01 to 0.1
Outputs:
- coupled_state: float32 [8, 256, 512, 256], P(None, 'rad', 'lon')
- drifted_density: float32 [128, 200, 128], P(('rad', 'lon'))
Inputs may be any that keep to these rules, and one draw needn't show every extreme that they name: `block_tile`: in each longitude sector and each aligned run of 64 radial rows, no tile is reached by more than 2 blocks. `tile_of_device`: every tile has exactly one owner.
All inputs are finite; a program needn't handle non-finite values.
Results may differ from a plain program's by a relative error of at most 0.000067.
Values sent between devices are 32-bit elements; how exact they have to be, the bound alone decides.
A program may use at most 192 MiB of HBM per device.

v0:
```python
import numpy as np

import jax
import jax.numpy as jnp
import ml_dtypes
from jax import lax
from jax.experimental import pallas as pl
from jax.experimental.pallas import tpu as pltpu
from jax.sharding import PartitionSpec as P

F32 = jnp.float32
BF16 = jnp.bfloat16
HIGHEST = lax.Precision.HIGHEST
MESH = pl.DeviceIdType.MESH

NF, CR, CL, CZ = 8, 64, 16, 256
ZSEG = 8
DRIFT = 3
CH, TP = 200, 128
NRAD, NLON = 4, 32
NYX, NZC = 16, 8
DEVICES = NRAD * NLON

SCALE = 0.4 * 0.5 / 30.0
ORDER = (0, 7, 1, 2, 3, 4, 5, 6)
ODD = {-3: -1.0, -2: 9.0, -1: -45.0, 1: 45.0, 2: -9.0, 3: 1.0}
EVEN = {-3: 1.0, -2: -6.0, -1: 15.0, 0: -20.0, 1: 15.0, 2: -6.0, 3: 1.0}

RB = 8
NB = CR // RB

C_FIX07, C_FIX, C_SEG, C_MASK, C_ODD, C_EVEN, C_EODD, C_EEVEN, C_END = (
    0, 128, 224, 480, 496, 512, 528, 576, 624
)


def constants():
    t = np.zeros((C_END, 128), np.float32)
    half = 64
    for c in range(2):
        for r in range(4):
            for l in range(CL):
                row = C_FIX07 + (c * 4 + r) * CL + l
                for h in range(2):
                    if l < 3:
                        t[row, h * half + r * 8 + 3 * c + l] = 1
                    if l >= CL - 3:
                        t[row, h * half + 32 + r * 8 + 3 * c + l - (CL - 3)] = 1
    for pos in range(2, NF):
        for l in range(CL):
            row = C_FIX + (pos - 2) * CL + l
            for h in range(2):
                if l < 3:
                    t[row, h * half + 3 * pos + l] = 1
                if l >= CL - 3:
                    t[row, h * half + 24 + 3 * pos + l - (CL - 3)] = 1
    for z in range(CZ):
        for p in range(TP):
            t[C_SEG + z, p] = z // (CZ // ZSEG) == p % ZSEG
    for l in range(CL):
        for p in range(TP):
            t[C_MASK + l, p] = p // ZSEG == l
    for l in range(CL):
        for f in range(NF):
            for j in range(CL):
                t[C_ODD + l, f * CL + j] = ODD.get(j - l, 0.0)
                t[C_EVEN + l, f * CL + j] = EVEN.get(j - l, 0.0)
    for side in range(2):
        for pos in range(NF):
            for k in range(3):
                row = side * 24 + 3 * pos + k
                for f in range(NF):
                    for j in range(CL):
                        off = j - CL - k if side == 0 else 3 + j - k
                        t[C_EODD + row, f * CL + j] = ODD.get(off, 0.0)
                        if f == ORDER[pos]:
                            t[C_EEVEN + row, f * CL + j] = EVEN.get(off, 0.0)
    return t.astype(ml_dtypes.bfloat16)


def split(x):
    hi = x.astype(BF16)
    return hi, (x - hi.astype(F32)).astype(BF16)


def kernel(
    state, volume, phase, matrices, speeds, targets, tiles, injection, courant, weight, table,
    out, drifted,
    cells, vol, dens, lhs, edge_lhs, send0, send1, recv0, recv1, rad_send, rad_recv,
    cols, pay, buf, ra, rb, rbs, g0, g1, g2,
    load_sem, vol_sem, dens_sem, lon_s0, lon_r0, lon_s1, lon_r1, rad_s, rad_r,
    ra_s, ra_r, rb_s, rb_r, g1_s, g1_r, g2_s, g2_r,
):
    rad, lon = lax.axis_index("rad"), lax.axis_index("lon")
    right, left = lax.rem(lon + 1, NLON), lax.rem(lon + NLON - 1, NLON)
    me_yx = rad * (NYX // NRAD) + lax.div(lon, NZC)
    me_zc = lax.rem(lon, NZC)

    def yx_peer(k):
        a = lax.rem(me_yx + k, NYX)
        return a, (lax.div(a, NYX // NRAD), lax.rem(a, NYX // NRAD) * NZC + me_zc)

    def zc_peer(k):
        i = lax.rem(me_zc + k, NZC)
        return i, (rad, lon - me_zc + i)

    def load(b):
        return pltpu.make_async_copy(
            state.at[:, pl.ds(b * RB, RB)], cells.at[:, pl.ds(3 + b * RB, RB)], load_sem.at[b]
        )

    for b in [0, NB - 1] + list(range(1, NB - 1)):
        load(b).start()
    vol_copy = pltpu.make_async_copy(volume, vol, vol_sem)
    vol_copy.start()
    dens_copy = pltpu.make_async_copy(phase, dens, dens_sem)
    dens_copy.start()

    barrier = pltpu.get_barrier_semaphore()

    def greet(device):
        pl.semaphore_signal(barrier, inc=1, device_id=device, device_id_type=MESH)

    greet((rad, right))
    greet((rad, left))
    for k in range(1, NYX):
        greet(yx_peer(k)[1])
    for k in range(1, NZC):
        greet(zc_peer(k)[1])

    cells[:, 0:3] = jnp.zeros((NF, 3, CL, CZ), F32)
    cells[:, 3 + CR :] = jnp.zeros((NF, 3, CL, CZ), F32)

    lane = lax.broadcasted_iota(jnp.int32, (CL, 128), 1)
    sub = lax.broadcasted_iota(jnp.int32, (CL, 128), 0)
    block = lax.shift_right_logical(lane, 4)
    same_l = jnp.bitwise_and(lane, CL - 1) == sub
    odd, even = table[C_ODD : C_ODD + CL].astype(F32), table[C_EVEN : C_EVEN + CL].astype(F32)
    rows_l = []
    for f in range(NF):
        row_r = jnp.zeros((CL, 128), F32)
        row_l = jnp.zeros((CL, 128), F32)
        for g in range(NF):
            row_r = jnp.where(block == g, matrices[0, f, g], row_r)
            row_l = jnp.where(block == g, matrices[1, f, g], row_l)
        rows_l.append(row_l)
        w = (SCALE * speeds[1]) * jnp.where(block == f, even, 0.0) - SCALE * row_l * odd
        whi, wlo = split(w)
        rhi, rlo = split(jnp.where(same_l, -SCALE * row_r, 0.0))
        at = f * CL
        lhs[at : at + CL, 0:128] = whi
        lhs[at : at + CL, 128:256] = rhi
        lhs[128 + at : 128 + at + CL, 0:128] = wlo
        lhs[128 + at : 128 + at + CL, 128:256] = rlo
    q = lax.broadcasted_iota(jnp.int32, (24, 128), 0)
    row_e = jnp.zeros((24, 128), F32)
    for pos, f in enumerate(ORDER):
        wide = jnp.concatenate([rows_l[f][0:8]] * 3, axis=0)
        row_e = jnp.where((q >= 3 * pos) & (q < 3 * pos + 3), wide, row_e)
    row_e = jnp.concatenate([row_e, row_e], axis=0)
    we = (SCALE * speeds[1]) * table[C_EEVEN : C_EEVEN + 48].astype(F32) - (
        SCALE * row_e * table[C_EODD : C_EODD + 48].astype(F32)
    )
    ehi, elo = split(we)
    edge_lhs[0:48, 0:128] = ehi
    edge_lhs[0:48, 128:256] = ehi
    edge_lhs[48:96, 0:128] = elo
    edge_lhs[48:96, 128:256] = jnp.zeros((48, 128), BF16)

    def row(i):
        return cells[:, i].reshape(NF * CL, CZ)

    load(0).wait()
    load(NB - 1).wait()

    def rad_edge(side):
        for k in range(3):
            d = jnp.zeros((128, CZ), F32)
            e = jnp.zeros((128, CZ), F32)
            for j in range(3):
                off = j - k - 3 if side == 0 else 3 + j - k
                if off in ODD:
                    u = row(CR + j if side == 0 else 3 + j)
                    d = d + ODD[off] * u
                    e = e + EVEN[off] * u
            dh, dl = split(d)
            y = (
                jnp.dot(lhs[0:128, 128:256], dh, preferred_element_type=F32)
                + jnp.dot(lhs[128:256, 128:256], dh, preferred_element_type=F32)
                + jnp.dot(lhs[0:128, 128:256], dl, preferred_element_type=F32)
                + (SCALE * speeds[0]) * e
            )
            for pos, f in enumerate(ORDER):
                rad_send[side, pos, k] = y[f * CL : (f + 1) * CL]

    def rad_copy(side, part):
        fields = pl.ds(0, 2) if part == 0 else pl.ds(2, NF - 2)
        return pltpu.make_async_remote_copy(
            src_ref=rad_send.at[side, fields],
            dst_ref=rad_recv.at[side, fields],
            send_sem=rad_s.at[side, part],
            recv_sem=rad_r.at[side, part],
            device_id=(rad + 1 if side == 0 else rad - 1, lon),
            device_id_type=MESH,
        )

    has = (rad < NRAD - 1, rad > 0)
    rad_edge(0)
    rad_edge(1)

    pl.semaphore_wait(barrier, 2 + NYX - 1 + NZC - 1)
    for side in range(2):
        @pl.when(has[side])
        def _():
            rad_copy(side, 0).start()

    def lon_copy(side, part, b):
        src, dst = (send0, recv0) if part == 0 else (send1, recv1)
        ss, rs = (lon_s0, lon_r0) if part == 0 else (lon_s1, lon_r1)
        rows = pl.ds(b * RB, RB)
        return pltpu.make_async_remote_copy(
            src_ref=src.at[side, rows],
            dst_ref=dst.at[side, rows],
            send_sem=ss.at[side, b],
            recv_sem=rs.at[side, b],
            device_id=(rad, right if side == 0 else left),
            device_id_type=MESH,
        )

    def edge_chunk(b, _):
        @pl.when((b > 0) & (b < NB - 1))
        def _():
            load(b).wait()

        def edge_row(i, _):
            r = b * RB + i
            hi, lo = split(row(3 + r))
            y = jnp.dot(
                edge_lhs[...], jnp.concatenate([hi, lo], axis=0), preferred_element_type=F32
            )
            y = y[0:48] + y[48:96]
            for side in range(2):
                send0[side, r] = y[side * 24 : side * 24 + 8]
                send1[side, r] = y[side * 24 + 8 : side * 24 + 24]
            return 0

        lax.fori_loop(0, RB, edge_row, 0, unroll=4)
        lon_copy(0, 0, b).start()
        lon_copy(1, 0, b).start()
        return 0

    lax.fori_loop(0, NB, edge_chunk, 0)

    def send_rest(b, _):
        lon_copy(0, 1, b).start()
        lon_copy(1, 1, b).start()
        return 0

    lax.fori_loop(0, NB, send_rest, 0)
    for side in range(2):
        @pl.when(has[side])
        def _():
            rad_copy(side, 1).start()

    def bulk(r, _):
        m3, m2, m1, u, p1, p2, p3 = (row(r + i) for i in range(7))
        d = 45.0 * (p1 - m1) - 9.0 * (p2 - m2) + (p3 - m3)
        e = 15.0 * (p1 + m1) - 6.0 * (p2 + m2) + (p3 + m3) - 20.0 * u
        xh, xl = split(u)
        dh, dl = split(d)
        t1 = jnp.concatenate([xh, dh], axis=0)
        t2 = jnp.concatenate([xl, dl], axis=0)
        y1 = jnp.dot(lhs[...], t1, preferred_element_type=F32)
        y2 = jnp.dot(lhs[0:128], t2, preferred_element_type=F32)
        new = u + (SCALE * speeds[0]) * e + (y1[0:128] + y1[128:256] + y2)
        out[:, r] = new.reshape(NF, CL, CZ)
        return 0

    lax.fori_loop(0, CR, bulk, 0, unroll=2)

    def add_rad(part):
        for side in range(2):
            @pl.when(has[1 - side])
            def _():
                rad_copy(side, part).wait_recv()
                for pos in range(2) if part == 0 else range(2, NF):
                    for k in range(3):
                        r = k if side == 0 else CR - 3 + k
                        out[ORDER[pos], r] = out[ORDER[pos], r] + rad_recv[side, pos, k]

    add_rad(0)
    vol_copy.wait()
    seg = table[C_SEG : C_SEG + CZ]
    mask = table[C_MASK : C_MASK + CL].astype(F32)

    def early(b, _):
        lon_copy(0, 0, b).wait_recv()
        lon_copy(1, 0, b).wait_recv()
        for h in range(RB // 4):
            r = b * RB + h * 4
            got = jnp.concatenate(
                [recv0[0, pl.ds(r, 4)].reshape(32, CZ), recv0[1, pl.ds(r, 4)].reshape(32, CZ)],
                axis=0,
            )
            hi, lo = split(got)
            add = jnp.dot(
                table[C_FIX07 : C_FIX07 + 128],
                jnp.concatenate([hi, lo], axis=0),
                preferred_element_type=F32,
            )
            v = vol[pl.ds(r, 4)].reshape(64, CZ)
            for c, f in enumerate((0, 7)):
                new = out[f, pl.ds(r, 4)].reshape(64, CZ) + add[c * 64 : (c + 1) * 64]
                out[f, pl.ds(r, 4)] = new.reshape(4, CL, CZ)
                yh, yl = split(v * new)
                t = jnp.dot(yh, seg, preferred_element_type=F32) + jnp.dot(
                    yl, seg, preferred_element_type=F32
                )
                t = t.reshape(4, CL, TP) * mask[None]
                pay[pl.ds(r * 8, 32), c * TP : (c + 1) * TP] = (t[:, 0:8] + t[:, 8:16]).reshape(
                    32, TP
                )
        return 0

    lax.fori_loop(0, NB, early, 0)

    hit = (targets[...] == tiles[...]).astype(F32)
    hit8 = jnp.broadcast_to(hit[:, None, :], (CR, 8, DEVICES)).reshape(CR * 8, DEVICES)
    buf[...] = lax.dot_general(
        hit8, pay[...], (((0,), (0,)), ((), ())), precision=HIGHEST, preferred_element_type=F32
    ).reshape(NYX, NZC, 2 * TP)

    def ra_copy(k):
        a, device = yx_peer(k)
        return pltpu.make_async_remote_copy(
            src_ref=buf.at[a], dst_ref=ra.at[k], send_sem=ra_s.at[k], recv_sem=ra_r.at[k],
            device_id=device, device_id_type=MESH,
        )

    def rb_copy(k):
        i, device = zc_peer(k)
        return pltpu.make_async_remote_copy(
            src_ref=rbs.at[i], dst_ref=rb.at[k], send_sem=rb_s.at[k], recv_sem=rb_r.at[k],
            device_id=device, device_id_type=MESH,
        )

    def g1_copy(k):
        i, device = zc_peer(k)
        return pltpu.make_async_remote_copy(
            src_ref=g0, dst_ref=g1.at[me_zc], send_sem=g1_s.at[k], recv_sem=g1_r.at[k],
            device_id=device, device_id_type=MESH,
        )

    def g2_copy(k):
        a, device = yx_peer(k)
        return pltpu.make_async_remote_copy(
            src_ref=g1, dst_ref=g2.at[me_yx], send_sem=g2_s.at[k], recv_sem=g2_r.at[k],
            device_id=device, device_id_type=MESH,
        )

    for k in range(1, NYX):
        ra_copy(k).start()
    total = buf[me_yx]
    cols[...] = jnp.zeros((8, 256), F32)
    cols[0:2, 0:CH] = injection[...]
    cols[2:3, 0:CH] = courant[...]
    cols[3:4, 0:CH] = weight[...]
    columns = cols[...].T
    dens_copy.wait()
    for k in range(1, NYX):
        ra_copy(k).wait_recv()
        total = total + ra[k]
    for i in range(NZC):
        rbs[i] = total[i : i + 1]
    for k in range(1, NZC):
        rb_copy(k).start()
    source = rbs[me_zc]
    for k in range(1, NZC):
        rb_copy(k).wait_recv()
        source = source + rb[k]

    density = dens[...] + 0.5 * (
        columns[0:CH, 0:1] * source[:, 0:TP] + columns[0:CH, 1:2] * source[:, TP:]
    )
    rate = jnp.broadcast_to(columns[0:CH, 2:3], (CH, TP))
    for _ in range(DRIFT):
        density = density - rate * (density - pltpu.roll(density, 1, axis=1))
    drifted[...] = density
    pressure = jnp.sum(columns[0:CH, 3:4] * density, axis=0, keepdims=True)
    g0[...] = pressure
    for k in range(1, NZC):
        g1_copy(k).start()
    g1[me_zc] = pressure
    for k in range(1, NZC):
        g1_copy(k).wait_recv()
    for k in range(1, NYX):
        g2_copy(k).start()
    g2[me_yx] = g1[...]

    add_rad(1)

    def late(b, _):
        lon_copy(0, 1, b).wait_recv()
        lon_copy(1, 1, b).wait_recv()

        def late_row(i, _):
            r = b * RB + i
            got = jnp.concatenate(
                [recv0[0, r], recv1[0, r], recv0[1, r], recv1[1, r], jnp.zeros((16, CZ), F32)],
                axis=0,
            )
            hi, lo = split(got)
            add = jnp.dot(
                table[C_FIX : C_FIX + 96],
                jnp.concatenate([hi, lo], axis=0),
                preferred_element_type=F32,
            )
            out[1:7, r] = out[1:7, r] + add.reshape(6, CL, CZ)
            return 0

        lax.fori_loop(0, RB, late_row, 0, unroll=4)
        return 0

    lax.fori_loop(0, NB, late, 0)

    for k in range(1, NYX):
        g2_copy(k).wait_recv()
    returned = jnp.dot(
        hit, g2[...].reshape(DEVICES, TP), precision=HIGHEST, preferred_element_type=F32
    )
    pay[0:CR, 0:TP] = returned

    def nudge(b, _):
        got = pay[pl.ds(b * RB, RB), 0:TP]
        wide = jnp.broadcast_to(got[:, None, :], (RB, CL, TP)) * mask[None]
        hi, lo = split(wide.reshape(RB * CL, TP))
        dims = (((1,), (1,)), ((), ()))
        back = lax.dot_general(hi, seg, dims, preferred_element_type=F32) + lax.dot_general(
            lo, seg, dims, preferred_element_type=F32
        )
        old = out[7, pl.ds(b * RB, RB)].reshape(RB * CL, CZ)
        out[7, pl.ds(b * RB, RB)] = (old + 0.5 * (back - old)).reshape(RB, CL, CZ)
        return 0

    lax.fori_loop(0, NB, nudge, 0)

    def sent(b, _):
        for side in range(2):
            for part in range(2):
                lon_copy(side, part, b).wait_send()
        return 0

    lax.fori_loop(0, NB, sent, 0)
    for side in range(2):
        @pl.when(has[side])
        def _():
            rad_copy(side, 0).wait_send()
            rad_copy(side, 1).wait_send()
    for k in range(1, NYX):
        ra_copy(k).wait_send()
        g2_copy(k).wait_send()
    for k in range(1, NZC):
        rb_copy(k).wait_send()
        g1_copy(k).wait_send()


def per_device(
    state, flux_matrices, wave_speed, flux_volume, block_tile, tile_of_device,
    phase_density, injection, drift_courant, energy_weight,
):
    any_spec = pl.BlockSpec(memory_space=pl.ANY)
    smem = pl.BlockSpec(memory_space=pltpu.SMEM)
    vmem = pl.BlockSpec(memory_space=pltpu.VMEM)
    dma = pltpu.SemaphoreType.DMA
    coupled, drifted = pl.pallas_call(
        kernel,
        out_shape=(
            pltpu.VMEM((NF, CR, CL, CZ), F32),
            jax.ShapeDtypeStruct((CH, TP), F32),
        ),
        in_specs=[any_spec] * 3 + [smem] * 2 + [vmem] * 6,
        out_specs=(vmem, vmem),
        scratch_shapes=[
            pltpu.VMEM((NF, CR + 6, CL, CZ), F32),
            pltpu.VMEM((CR, CL, CZ), F32),
            pltpu.VMEM((CH, TP), F32),
            pltpu.VMEM((256, 256), BF16),
            pltpu.VMEM((96, 256), BF16),
            pltpu.VMEM((2, CR, 8, CZ), F32),
            pltpu.VMEM((2, CR, 16, CZ), F32),
            pltpu.VMEM((2, CR, 8, CZ), F32),
            pltpu.VMEM((2, CR, 16, CZ), F32),
            pltpu.VMEM((2, NF, 3, CL, CZ), F32),
            pltpu.VMEM((2, NF, 3, CL, CZ), F32),
            pltpu.VMEM((8, 256), F32),
            pltpu.VMEM((CR * 8, 2 * TP), F32),
            pltpu.VMEM((NYX, NZC, 2 * TP), F32),
            pltpu.VMEM((NYX, NZC, 2 * TP), F32),
            pltpu.VMEM((NZC, 1, 2 * TP), F32),
            pltpu.VMEM((NZC, 1, 2 * TP), F32),
            pltpu.VMEM((1, TP), F32),
            pltpu.VMEM((NZC, 1, TP), F32),
            pltpu.VMEM((NYX, NZC, 1, TP), F32),
            dma((NB,)), dma, dma,
            dma((2, NB)), dma((2, NB)), dma((2, NB)), dma((2, NB)),
            dma((2, 2)), dma((2, 2)),
            dma((NYX,)), dma((NYX,)), dma((NZC,)), dma((NZC,)),
            dma((NZC,)), dma((NZC,)), dma((NYX,)), dma((NYX,)),
        ],
        compiler_params=pltpu.CompilerParams(
            collective_id=0, has_side_effects=True, vmem_limit_bytes=40 << 20
        ),
    )(
        state,
        flux_volume,
        phase_density.reshape(CH, TP),
        flux_matrices,
        wave_speed,
        block_tile.reshape(CR, 1),
        tile_of_device.reshape(1, DEVICES),
        injection,
        drift_courant.reshape(1, CH),
        energy_weight.reshape(1, CH),
        jnp.asarray(constants()),
    )
    return coupled, drifted[None]


def solution(mesh):
    in_specs = (
        P(None, "rad", "lon", None),
        P(),
        P(),
        P("rad", "lon", None),
        P("lon", "rad", None),
        P(),
        P(("rad", "lon"), None, None),
        P(),
        P(),
        P(),
    )
    out_specs = (P(None, "rad", "lon", None), P(("rad", "lon"), None, None))
    return jax.shard_map(
        per_device, mesh=mesh, in_specs=in_specs, out_specs=out_specs, check_vma=False
    )
```

profile of v0, /device:TPU:1, one launch (start us, length us, event | category | flops | bytes accessed | tf_op | source)
XLA Modules:
  0.0 60.9 jit_solution(14350372572667523088)
XLA Ops:
  0.6 0.7 %copy.13.targets = s32[64,1]{1,0:T(8,128)S(1)} copy(s32[64,1]{0,1:T(1,128)} %bitcast.11) | data formatting | bytes 512 | tf_op jit(solution)/shard_map/reshape | solution.py:519
  1.4 0.0 copy-start
  1.4 1.2 %copy-done = f32[64,16,256]{2,1,0:T(8,128)S(1)} copy-done((f32[64,16,256]{2,1,0:T(8,128)S(1)}, f32[64,16,256]{2,1,0:T(8,128)}, u32[]{:S(2)}) %copy-start) | copy-done | bytes 1048600
  2.6 0.0 copy-start.1
  2.6 0.9 %copy-done.1 = bf16[624,128]{1,0:T(8,128)(2,1)S(1)} copy-done((bf16[624,128]{1,0:T(8,128)(2,1)S(1)}, bf16[624,128]{1,0:T(8,128)(2,1)}, u32[]{:S(2)}) %copy-start.1) | copy-done | bytes 159768
  3.5 0.0 copy-start.2
  3.5 0.9 %copy-done.2 = f32[1,200,128]{2,1,0:T(8,128)S(1)} copy-done((f32[1,200,128]{2,1,0:T(8,128)S(1)}, f32[1,200,128]{2,1,0:T(8,128)}, u32[]{:S(2)}) %copy-start.2) | copy-done | bytes 102424
  4.4 0.0 copy-start.3
  4.4 0.7 %copy-done.3 = f32[2,8,8]{2,1,0:T(8,128)S(1)} copy-done((f32[2,8,8]{2,1,0:T(8,128)S(1)}, f32[2,8,8]{2,1,0:T(8,128)}, u32[]{:S(2)}) %copy-start.3) | copy-done | bytes 536
  5.1 0.0 copy-start.4
  5.1 0.7 %copy-done.4 = f32[2,200]{1,0:T(2,128)S(1)} copy-done((f32[2,200]{1,0:T(2,128)S(1)}, f32[2,200]{1,0:T(2,128)}, u32[]{:S(2)}) %copy-start.4) | copy-done | bytes 1624
  5.8 0.0 copy-start.5
  5.8 0.7 %copy-done.5 = f32[200]{0:T(256)S(1)} copy-done((f32[200]{0:T(256)S(1)}, f32[200]{0:T(256)}, u32[]{:S(2)}) %copy-start.5) | copy-done | bytes 824
  6.5 0.0 copy-start.6
  6.5 0.7 %copy-done.6 = f32[200]{0:T(256)S(1)} copy-done((f32[200]{0:T(256)S(1)}, f32[200]{0:T(256)}, u32[]{:S(2)}) %copy-start.6) | copy-done | bytes 824
  7.1 0.0 copy-start.7
  7.2 0.7 %copy-done.7 = f32[2]{0:T(128)S(1)} copy-done((f32[2]{0:T(128)S(1)}, f32[2]{0:T(128)}, u32[]{:S(2)}) %copy-start.7) | copy-done | bytes 32
  7.8 0.0 copy-start.8
  7.8 0.7 %copy-done.8 = s32[128]{0:T(128)S(1)} copy-done((s32[128]{0:T(128)S(1)}, s32[128]{0:T(128)}, u32[]{:S(2)}) %copy-start.8) | copy-done | bytes 536
  8.5 48.4 %shard_map.122 = (f32[8,64,16,256]{3,2,1,0:T(8,128)S(1)}, f32[200,128]{1,0:T(8,128)S(1)}) custom-call(f32[8,64,16,256]{3,2,1,0:T(8,128)} %state.1, f32[64,16,256]{2,1,0:T(8,128)S(1)} %copy-done, f32[200,128]{1,0:T(8,128)S(1)} %bitcast.7, f32[2,8,8]{2,1,0:T(8,128)S(1)} %copy-done.3, f32[2]{0:T(128)S(1)} %copy-done.7, s32[64,1]{1,0:T(8,128)S(1)} %copy.13.targets, ...), custom_call_target="tpu_custom_call" | custom-call | tf_op jit(solution)/shard_map/pallas_call | solution.py:475
  56.9 3.4 %copy.16 = f32[8,64,16,256]{3,2,1,0:T(8,128)} copy(f32[8,64,16,256]{3,2,1,0:T(8,128)S(1)} %get-tuple-element.6) | data formatting | bytes 16777216
  60.3 0.6 %copy.17 = f32[1,200,128]{2,1,0:T(8,128)} copy(f32[1,200,128]{2,1,0:T(8,128)S(1)} %bitcast.6) | data formatting | bytes 204800
Async XLA Ops:
  1.4 1.2 %copy-start = (f32[64,16,256]{2,1,0:T(8,128)S(1)}, f32[64,16,256]{2,1,0:T(8,128)}, u32[]{:S(2)}) copy-start(f32[64,16,256]{2,1,0:T(8,128)} %volume.1) | copy-start | bytes 3145732
  2.6 0.9 %copy-start.1 = (bf16[624,128]{1,0:T(8,128)(2,1)S(1)}, bf16[624,128]{1,0:T(8,128)(2,1)}, u32[]{:S(2)}) copy-start(bf16[624,128]{1,0:T(8,128)(2,1)} %constant.2.clone.table) | copy-start | bytes 479236
  3.5 0.9 %copy-start.2 = (f32[1,200,128]{2,1,0:T(8,128)S(1)}, f32[1,200,128]{2,1,0:T(8,128)}, u32[]{:S(2)}) copy-start(f32[1,200,128]{2,1,0:T(8,128)} %param.17) | copy-start | bytes 307204
  4.4 0.7 %copy-start.3 = (f32[2,8,8]{2,1,0:T(8,128)S(1)}, f32[2,8,8]{2,1,0:T(8,128)}, u32[]{:S(2)}) copy-start(f32[2,8,8]{2,1,0:T(8,128)} %matrices.1) | copy-start | bytes 1540
  5.1 0.7 %copy-start.4 = (f32[2,200]{1,0:T(2,128)S(1)}, f32[2,200]{1,0:T(2,128)}, u32[]{:S(2)}) copy-start(f32[2,200]{1,0:T(2,128)} %injection.1) | copy-start | bytes 4804
  5.8 0.7 %copy-start.5 = (f32[200]{0:T(256)S(1)}, f32[200]{0:T(256)}, u32[]{:S(2)}) copy-start(f32[200]{0:T(256)} %param.19) | copy-start | bytes 2404
  6.5 0.7 %copy-start.6 = (f32[200]{0:T(256)S(1)}, f32[200]{0:T(256)}, u32[]{:S(2)}) copy-start(f32[200]{0:T(256)} %param.20) | copy-start | bytes 2404
  7.1 0.7 %copy-start.7 = (f32[2]{0:T(128)S(1)}, f32[2]{0:T(128)}, u32[]{:S(2)}) copy-start(f32[2]{0:T(128)} %speeds.1) | copy-start | bytes 28
  7.8 0.7 %copy-start.8 = (s32[128]{0:T(128)S(1)}, s32[128]{0:T(128)}, u32[]{:S(2)}) copy-start(s32[128]{0:T(128)} %param.16) | copy-start | bytes 1540
where the time goes:
time: 61.4 us; the launch traced here: 60.9 us
  Pallas kernels  48.4 us (79%)
  local copies, waits for them, and re-layouts  11.9 us (19%)
  between operations  0.65 us (1%)
    pallas_call x1, Pallas kernels, per_device(): pl.pallas_call(kernel, out_shape=(pltpu.VMEM((NF, CR, CL, CZ), F32), jax....  48.4 us
    unnamed x20, local copies, waits for them, and re-layouts  11.1 us

commit v1 on v0

--- a/solution.py
+++ b/solution.py
@@ -28,6 +28,7 @@
 
 RB = 8
 NB = CR // RB
+AHEAD = 4
 
 C_FIX07, C_FIX, C_SEG, C_MASK, C_ODD, C_EVEN, C_EODD, C_EEVEN, C_END = (
     0, 128, 224, 480, 496, 512, 528, 576, 624
@@ -84,12 +85,13 @@
 
 
 def kernel(
-    state, volume, phase, matrices, speeds, targets, tiles, injection, courant, weight, table,
+    state, volume, phase, matrices_in, speeds_in, targets_in, tiles_in, injection, courant, weight,
+    table_in,
     out, drifted,
-    cells, vol, dens, lhs, edge_lhs, send0, send1, recv0, recv1, rad_send, rad_recv,
-    cols, pay, buf, ra, rb, rbs, g0, g1, g2,
-    load_sem, vol_sem, dens_sem, lon_s0, lon_r0, lon_s1, lon_r1, rad_s, rad_r,
-    ra_s, ra_r, rb_s, rb_r, g1_s, g1_r, g2_s, g2_r,
+    matrices, speeds, targets, tiles, table, inj, cou, wei, cells, vol, dens, lhs, send0, send1,
+    recv0, recv1, rad_send, rad_recv, cols, pay, hit_db, hit_bd, buf, ra, part, rb, p0, g0, g2,
+    small_sem, load_sem, vol_sem, dens_sem, lon_s0, lon_r0, lon_s1, lon_r1, rad_s, rad_r,
+    p0_s, p0_r, ra_s, ra_r, rb_s, rb_r, g2_s, g2_r,
 ):
     rad, lon = lax.axis_index("rad"), lax.axis_index("lon")
     right, left = lax.rem(lon + 1, NLON), lax.rem(lon + NLON - 1, NLON)
@@ -104,12 +106,23 @@
         i = lax.rem(me_zc + k, NZC)
         return i, (rad, lon - me_zc + i)
 
+    small = [
+        pltpu.make_async_copy(src, dst, small_sem.at[i])
+        for i, (src, dst) in enumerate((
+            (matrices_in, matrices), (speeds_in, speeds), (table_in, table),
+            (targets_in, targets), (tiles_in, tiles),
+            (injection, inj), (courant, cou), (weight, wei),
+        ))
+    ]
+    for copy in small:
+        copy.start()
+
     def load(b):
         return pltpu.make_async_copy(
             state.at[:, pl.ds(b * RB, RB)], cells.at[:, pl.ds(3 + b * RB, RB)], load_sem.at[b]
         )
 
-    for b in [0, NB - 1] + list(range(1, NB - 1)):
+    for b in [0, 1, NB - 1] + list(range(2, NB - 1)):
         load(b).start()
     vol_copy = pltpu.make_async_copy(volume, vol, vol_sem)
     vol_copy.start()
@@ -131,6 +144,8 @@
     cells[:, 0:3] = jnp.zeros((NF, 3, CL, CZ), F32)
     cells[:, 3 + CR :] = jnp.zeros((NF, 3, CL, CZ), F32)
 
+    for copy in small:
+        copy.wait()
     lane = lax.broadcasted_iota(jnp.int32, (CL, 128), 1)
     sub = lax.broadcasted_iota(jnp.int32, (CL, 128), 0)
     block = lax.shift_right_logical(lane, 4)
@@ -144,14 +159,19 @@
             row_r = jnp.where(block == g, matrices[0, f, g], row_r)
             row_l = jnp.where(block == g, matrices[1, f, g], row_l)
         rows_l.append(row_l)
-        w = (SCALE * speeds[1]) * jnp.where(block == f, even, 0.0) - SCALE * row_l * odd
+        eye = lane == sub + f * CL
+        w = (
+            (SCALE * speeds[1]) * jnp.where(block == f, even, 0.0)
+            - SCALE * row_l * odd
+            + jnp.where(eye, 1.0 - 20.0 * SCALE * speeds[0], 0.0)
+        )
         whi, wlo = split(w)
-        rhi, rlo = split(jnp.where(same_l, -SCALE * row_r, 0.0))
+        rhi, rlo = split(jnp.where(same_l, (-45.0 * SCALE) * row_r, 0.0))
         at = f * CL
-        lhs[at : at + CL, 0:128] = whi
-        lhs[at : at + CL, 128:256] = rhi
-        lhs[128 + at : 128 + at + CL, 0:128] = wlo
-        lhs[128 + at : 128 + at + CL, 128:256] = rlo
+        lhs[at : at + CL, 0:128] = wlo
+        lhs[at : at + CL, 128:256] = rlo
+        lhs[128 + at : 128 + at + CL, 0:128] = whi
+        lhs[128 + at : 128 + at + CL, 128:256] = rhi
     q = lax.broadcasted_iota(jnp.int32, (24, 128), 0)
     row_e = jnp.zeros((24, 128), F32)
     for pos, f in enumerate(ORDER):
@@ -162,16 +182,12 @@
         SCALE * row_e * table[C_EODD : C_EODD + 48].astype(F32)
     )
     ehi, elo = split(we)
-    edge_lhs[0:48, 0:128] = ehi
-    edge_lhs[0:48, 128:256] = ehi
-    edge_lhs[48:96, 0:128] = elo
-    edge_lhs[48:96, 128:256] = jnp.zeros((48, 128), BF16)
+    lhs[256:304, 0:128] = ehi
+    lhs[304:352, 0:128] = elo
+    lhs[256:352, 128:256] = jnp.zeros((96, 128), BF16)
 
     def row(i):
         return cells[:, i].reshape(NF * CL, CZ)
-
-    load(0).wait()
-    load(NB - 1).wait()
 
     def rad_edge(side):
         for k in range(3):
@@ -181,13 +197,13 @@
                 off = j - k - 3 if side == 0 else 3 + j - k
                 if off in ODD:
                     u = row(CR + j if side == 0 else 3 + j)
-                    d = d + ODD[off] * u
+                    d = d + (ODD[off] / 45.0) * u
                     e = e + EVEN[off] * u
             dh, dl = split(d)
             y = (
                 jnp.dot(lhs[0:128, 128:256], dh, preferred_element_type=F32)
                 + jnp.dot(lhs[128:256, 128:256], dh, preferred_element_type=F32)
-                + jnp.dot(lhs[0:128, 128:256], dl, preferred_element_type=F32)
+                + jnp.dot(lhs[128:256, 128:256], dl, preferred_element_type=F32)
                 + (SCALE * speeds[0]) * e
             )
             for pos, f in enumerate(ORDER):
@@ -205,14 +221,6 @@
         )
 
     has = (rad < NRAD - 1, rad > 0)
-    rad_edge(0)
-    rad_edge(1)
-
-    pl.semaphore_wait(barrier, 2 + NYX - 1 + NZC - 1)
-    for side in range(2):
-        @pl.when(has[side])
-        def _():
-            rad_copy(side, 0).start()
 
     def lon_copy(side, part, b):
         src, dst = (send0, recv0) if part == 0 else (send1, recv1)
@@ -227,56 +235,119 @@
             device_id_type=MESH,
         )
 
-    def edge_chunk(b, _):
-        @pl.when((b > 0) & (b < NB - 1))
-        def _():
-            load(b).wait()
-
-        def edge_row(i, _):
-            r = b * RB + i
-            hi, lo = split(row(3 + r))
-            y = jnp.dot(
-                edge_lhs[...], jnp.concatenate([hi, lo], axis=0), preferred_element_type=F32
-            )
-            y = y[0:48] + y[48:96]
-            for side in range(2):
-                send0[side, r] = y[side * 24 : side * 24 + 8]
-                send1[side, r] = y[side * 24 + 8 : side * 24 + 24]
-            return 0
-
-        lax.fori_loop(0, RB, edge_row, 0, unroll=4)
-        lon_copy(0, 0, b).start()
-        lon_copy(1, 0, b).start()
-        return 0
-
-    lax.fori_loop(0, NB, edge_chunk, 0)
-
-    def send_rest(b, _):
-        lon_copy(0, 1, b).start()
-        lon_copy(1, 1, b).start()
-        return 0
-
-    lax.fori_loop(0, NB, send_rest, 0)
-    for side in range(2):
-        @pl.when(has[side])
-        def _():
-            rad_copy(side, 1).start()
-
     def bulk(r, _):
         m3, m2, m1, u, p1, p2, p3 = (row(r + i) for i in range(7))
-        d = 45.0 * (p1 - m1) - 9.0 * (p2 - m2) + (p3 - m3)
-        e = 15.0 * (p1 + m1) - 6.0 * (p2 + m2) + (p3 + m3) - 20.0 * u
+        d = (p1 - m1) - 0.2 * ((p2 - m2) - (1.0 / 9.0) * (p3 - m3))
+        e = (p1 + m1) - 0.4 * ((p2 + m2) - (1.0 / 6.0) * (p3 + m3))
         xh, xl = split(u)
         dh, dl = split(d)
         t1 = jnp.concatenate([xh, dh], axis=0)
         t2 = jnp.concatenate([xl, dl], axis=0)
         y1 = jnp.dot(lhs[...], t1, preferred_element_type=F32)
-        y2 = jnp.dot(lhs[0:128], t2, preferred_element_type=F32)
-        new = u + (SCALE * speeds[0]) * e + (y1[0:128] + y1[128:256] + y2)
+        y2 = jnp.dot(lhs[128:304], t2, preferred_element_type=F32)
+        new = (y1[0:128] + y1[128:256] + y2[0:128]) + (15.0 * SCALE * speeds[0]) * e
         out[:, r] = new.reshape(NF, CL, CZ)
+        edge = y1[256:304] + y1[304:352] + y2[128:176]
+        for side in range(2):
+            send0[side, r] = edge[side * 24 : side * 24 + 8]
+            send1[side, r] = edge[side * 24 + 8 : side * 24 + 24]
         return 0
 
-    lax.fori_loop(0, CR, bulk, 0, unroll=2)
+    def bulk_chunk(b):
+        lax.fori_loop(0, RB, lambda i, _: bulk(b * RB + i, _), 0, unroll=4)
+
+    def send_early(b):
+        lon_copy(0, 0, b).start()
+        lon_copy(1, 0, b).start()
+
+    def send_late(b, _):
+        lon_copy(0, 1, b).start()
+        lon_copy(1, 1, b).start()
+        return 0
+
+    load(0).wait()
+    load(1).wait()
+    bulk_chunk(0)
+    pl.semaphore_wait(barrier, 2 + NYX - 1 + NZC - 1)
+    send_early(0)
+    load(NB - 1).wait()
+    rad_edge(0)
+    rad_edge(1)
+    for part_of in range(2):
+        for side in range(2):
+            @pl.when(has[side])
+            def _():
+                rad_copy(side, part_of).start()
+
+    cols[...] = jnp.zeros((8, 256), F32)
+    cols[0:2, 0:CH] = inj[...]
+    cols[2:3, 0:CH] = cou[...]
+    cols[3:4, 0:CH] = wei[...]
+    columns = cols[...].T
+    channel_rate = jnp.broadcast_to(columns[0:CH, 2:3], (CH, TP))
+    channel_weight = jnp.broadcast_to(columns[0:CH, 3:4], (CH, TP))
+
+    def drift(density):
+        for _ in range(DRIFT):
+            density = density - channel_rate * (density - pltpu.roll(density, 1, axis=1))
+        return density
+
+    def moment(density):
+        return jnp.sum(channel_weight * density, axis=0, keepdims=True)
+
+    def p0_copy(k):
+        i, device = zc_peer(k)
+        return pltpu.make_async_remote_copy(
+            src_ref=p0.at[me_zc], dst_ref=p0.at[me_zc], send_sem=p0_s.at[k],
+            recv_sem=p0_r.at[k], device_id=device, device_id_type=MESH,
+        )
+
+    dens_copy.wait()
+    p0[me_zc] = moment(drift(dens[...]))
+    for k in range(1, NZC):
+        p0_copy(k).start()
+
+    rate_row, weight_row = cols[2:3], cols[3:4]
+    keep = 1.0 - rate_row
+    powers = (
+        keep * keep * keep,
+        3.0 * keep * keep * rate_row,
+        3.0 * keep * rate_row * rate_row,
+        rate_row * rate_row * rate_row,
+    )
+    taps = [
+        [
+            jnp.sum(0.5 * weight_row * cols[i : i + 1] * power, axis=1, keepdims=True)
+            for power in powers
+        ]
+        for i in range(2)
+    ]
+
+    tile_col = jnp.broadcast_to(tiles[...].astype(F32), (DEVICES, DEVICES)).T
+    target_row = jnp.broadcast_to(targets[...].astype(F32), (DEVICES, CR))
+    hit = (tile_col[:, 0:CR] == target_row).astype(BF16)
+    spread = lax.shift_right_logical(
+        lax.broadcasted_iota(jnp.int32, (CR, CR * 8), 1), 3
+    ) == lax.broadcasted_iota(jnp.int32, (CR, CR * 8), 0)
+    hit_db[...] = jnp.dot(
+        hit, spread.astype(F32).astype(BF16), preferred_element_type=F32
+    ).astype(BF16)
+    target_col = jnp.concatenate(
+        [target_row, jnp.zeros((DEVICES, DEVICES - CR), F32)], axis=1
+    ).T
+    hit_bd[...] = (target_col[0:CR] == tiles[...].astype(F32)).astype(F32).astype(BF16)
+
+    def rest(b, _):
+        @pl.when(b < NB - 2)
+        def _():
+            load(b + 1).wait()
+
+        bulk_chunk(b)
+        send_early(b)
+        return 0
+
+    lax.fori_loop(1, NB, rest, 0)
+    lax.fori_loop(0, AHEAD, send_late, 0)
 
     def add_rad(part):
         for side in range(2):
@@ -294,10 +365,11 @@
     mask = table[C_MASK : C_MASK + CL].astype(F32)
 
     def early(b, _):
-        lon_copy(0, 0, b).wait_recv()
-        lon_copy(1, 0, b).wait_recv()
-        for h in range(RB // 4):
-            r = b * RB + h * 4
+        for i in range(2):
+            lon_copy(0, 0, 2 * b + i).wait_recv()
+            lon_copy(1, 0, 2 * b + i).wait_recv()
+        for h in range(2 * RB // 4):
+            r = b * 2 * RB + h * 4
             got = jnp.concatenate(
                 [recv0[0, pl.ds(r, 4)].reshape(32, CZ), recv0[1, pl.ds(r, 4)].reshape(32, CZ)],
                 axis=0,
@@ -322,12 +394,12 @@
                 )
         return 0
 
-    lax.fori_loop(0, NB, early, 0)
-
-    hit = (targets[...] == tiles[...]).astype(F32)
-    hit8 = jnp.broadcast_to(hit[:, None, :], (CR, 8, DEVICES)).reshape(CR * 8, DEVICES)
-    buf[...] = lax.dot_general(
-        hit8, pay[...], (((0,), (0,)), ((), ())), precision=HIGHEST, preferred_element_type=F32
+    lax.fori_loop(0, NB // 2, early, 0)
+
+    pay_hi, pay_lo = split(pay[...])
+    buf[...] = (
+        jnp.dot(hit_db[...], pay_hi, preferred_element_type=F32)
+        + jnp.dot(hit_db[...], pay_lo, preferred_element_type=F32)
     ).reshape(NYX, NZC, 2 * TP)
 
     def ra_copy(k):
@@ -340,64 +412,16 @@
     def rb_copy(k):
         i, device = zc_peer(k)
         return pltpu.make_async_remote_copy(
-            src_ref=rbs.at[i], dst_ref=rb.at[k], send_sem=rb_s.at[k], recv_sem=rb_r.at[k],
-            device_id=device, device_id_type=MESH,
-        )
-
-    def g1_copy(k):
-        i, device = zc_peer(k)
-        return pltpu.make_async_remote_copy(
-            src_ref=g0, dst_ref=g1.at[me_zc], send_sem=g1_s.at[k], recv_sem=g1_r.at[k],
+            src_ref=part, dst_ref=rb.at[k], send_sem=rb_s.at[k], recv_sem=rb_r.at[k],
             device_id=device, device_id_type=MESH,
         )
 
     def g2_copy(k):
         a, device = yx_peer(k)
         return pltpu.make_async_remote_copy(
-            src_ref=g1, dst_ref=g2.at[me_yx], send_sem=g2_s.at[k], recv_sem=g2_r.at[k],
+            src_ref=g0, dst_ref=g2.at[me_yx], send_sem=g2_s.at[k], recv_sem=g2_r.at[k],
             device_id=device, device_id_type=MESH,
         )
-
-    for k in range(1, NYX):
-        ra_copy(k).start()
-    total = buf[me_yx]
-    cols[...] = jnp.zeros((8, 256), F32)
-    cols[0:2, 0:CH] = injection[...]
-    cols[2:3, 0:CH] = courant[...]
-    cols[3:4, 0:CH] = weight[...]
-    columns = cols[...].T
-    dens_copy.wait()
-    for k in range(1, NYX):
-        ra_copy(k).wait_recv()
-        total = total + ra[k]
-    for i in range(NZC):
-        rbs[i] = total[i : i + 1]
-    for k in range(1, NZC):
-        rb_copy(k).start()
-    source = rbs[me_zc]
-    for k in range(1, NZC):
-        rb_copy(k).wait_recv()
-        source = source + rb[k]
-
-    density = dens[...] + 0.5 * (
-        columns[0:CH, 0:1] * source[:, 0:TP] + columns[0:CH, 1:2] * source[:, TP:]
-    )
-    rate = jnp.broadcast_to(columns[0:CH, 2:3], (CH, TP))
-    for _ in range(DRIFT):
-        density = density - rate * (density - pltpu.roll(density, 1, axis=1))
-    drifted[...] = density
-    pressure = jnp.sum(columns[0:CH, 3:4] * density, axis=0, keepdims=True)
-    g0[...] = pressure
-    for k in range(1, NZC):
-        g1_copy(k).start()
-    g1[me_zc] = pressure
-    for k in range(1, NZC):
-        g1_copy(k).wait_recv()
-    for k in range(1, NYX):
-        g2_copy(k).start()
-    g2[me_yx] = g1[...]
-
-    add_rad(1)
 
     def late(b, _):
         lon_copy(0, 1, b).wait_recv()
@@ -418,17 +442,52 @@
             out[1:7, r] = out[1:7, r] + add.reshape(6, CL, CZ)
             return 0
 
-        lax.fori_loop(0, RB, late_row, 0, unroll=4)
+        lax.fori_loop(0, RB, late_row, 0, unroll=8)
         return 0
 
-    lax.fori_loop(0, NB, late, 0)
+    for k in range(1, NYX):
+        ra_copy(k).start()
+    add_rad(1)
+    lax.fori_loop(0, 2, late, 0)
+    total = buf[me_yx]
+    for k in range(1, NYX):
+        ra_copy(k).wait_recv()
+        total = total + ra[k]
+    part[...] = total
+    for k in range(1, NZC):
+        rb_copy(k).start()
+    lax.fori_loop(AHEAD, NB, send_late, 0)
+    lax.fori_loop(2, AHEAD, late, 0)
+    source = part[...]
+    for k in range(1, NZC):
+        rb_copy(k).wait_recv()
+        source = source + rb[k]
+    for k in range(1, NZC):
+        p0_copy(k).wait_recv()
+    pressure = p0[...].reshape(NZC, TP)
+    for i in range(2):
+        s = source[:, i * TP : (i + 1) * TP]
+        for n in range(4):
+            pressure = pressure + taps[i][n] * (pltpu.roll(s, n, axis=1) if n else s)
+    g0[...] = pressure
+    for k in range(1, NYX):
+        g2_copy(k).start()
+    g2[me_yx] = pressure
+
+    own = lax.broadcasted_iota(jnp.int32, (NZC, 2 * TP), 0) == me_zc
+    mine = jnp.sum(jnp.where(own, source, 0.0), axis=0, keepdims=True)
+    drifted[...] = drift(
+        dens[...]
+        + 0.5 * (columns[0:CH, 0:1] * mine[:, 0:TP] + columns[0:CH, 1:2] * mine[:, TP:])
+    )
+    lax.fori_loop(AHEAD, NB - 1, late, 0)
 
     for k in range(1, NYX):
         g2_copy(k).wait_recv()
-    returned = jnp.dot(
-        hit, g2[...].reshape(DEVICES, TP), precision=HIGHEST, preferred_element_type=F32
+    back_hi, back_lo = split(g2[...].reshape(DEVICES, TP))
+    pay[0:CR, 0:TP] = jnp.dot(hit_bd[...], back_hi, preferred_element_type=F32) + jnp.dot(
+        hit_bd[...], back_lo, preferred_element_type=F32
     )
-    pay[0:CR, 0:TP] = returned
 
     def nudge(b, _):
         got = pay[pl.ds(b * RB, RB), 0:TP]
@@ -443,6 +502,7 @@
         return 0
 
     lax.fori_loop(0, NB, nudge, 0)
+    lax.fori_loop(NB - 1, NB, late, 0)
 
     def sent(b, _):
         for side in range(2):
@@ -461,31 +521,47 @@
         g2_copy(k).wait_send()
     for k in range(1, NZC):
         rb_copy(k).wait_send()
-        g1_copy(k).wait_send()
+        p0_copy(k).wait_send()
+
+
+def finish(fields, density, fields_out, density_out, sem):
+    copies = [
+        pltpu.make_async_copy(fields.at[f], fields_out.at[f], sem.at[f]) for f in range(NF)
+    ] + [pltpu.make_async_copy(density, density_out, sem.at[NF])]
+    for copy in copies:
+        copy.start()
+    for copy in copies:
+        copy.wait()
 
 
 def per_device(
     state, flux_matrices, wave_speed, flux_volume, block_tile, tile_of_device,
     phase_density, injection, drift_courant, energy_weight,
 ):
-    any_spec = pl.BlockSpec(memory_space=pl.ANY)
-    smem = pl.BlockSpec(memory_space=pltpu.SMEM)
+    hbm = pl.BlockSpec(memory_space=pltpu.HBM)
     vmem = pl.BlockSpec(memory_space=pltpu.VMEM)
     dma = pltpu.SemaphoreType.DMA
     coupled, drifted = pl.pallas_call(
         kernel,
         out_shape=(
             pltpu.VMEM((NF, CR, CL, CZ), F32),
-            jax.ShapeDtypeStruct((CH, TP), F32),
+            pltpu.VMEM((CH, TP), F32),
         ),
-        in_specs=[any_spec] * 3 + [smem] * 2 + [vmem] * 6,
+        in_specs=[hbm] * 11,
         out_specs=(vmem, vmem),
         scratch_shapes=[
+            pltpu.SMEM((2, NF, NF), F32),
+            pltpu.SMEM((2,), F32),
+            pltpu.VMEM((1, CR), jnp.int32),
+            pltpu.VMEM((1, DEVICES), jnp.int32),
+            pltpu.VMEM((C_END, 128), BF16),
+            pltpu.VMEM((2, CH), F32),
+            pltpu.VMEM((1, CH), F32),
+            pltpu.VMEM((1, CH), F32),
             pltpu.VMEM((NF, CR + 6, CL, CZ), F32),
             pltpu.VMEM((CR, CL, CZ), F32),
             pltpu.VMEM((CH, TP), F32),
-            pltpu.VMEM((256, 256), BF16),
-            pltpu.VMEM((96, 256), BF16),
+            pltpu.VMEM((352, 256), BF16),
             pltpu.VMEM((2, CR, 8, CZ), F32),
             pltpu.VMEM((2, CR, 16, CZ), F32),
             pltpu.VMEM((2, CR, 8, CZ), F32),
@@ -494,21 +570,23 @@
             pltpu.VMEM((2, NF, 3, CL, CZ), F32),
             pltpu.VMEM((8, 256), F32),
             pltpu.VMEM((CR * 8, 2 * TP), F32),
+            pltpu.VMEM((DEVICES, CR * 8), BF16),
+            pltpu.VMEM((CR, DEVICES), BF16),
             pltpu.VMEM((NYX, NZC, 2 * TP), F32),
             pltpu.VMEM((NYX, NZC, 2 * TP), F32),
-            pltpu.VMEM((NZC, 1, 2 * TP), F32),
-            pltpu.VMEM((NZC, 1, 2 * TP), F32),
-            pltpu.VMEM((1, TP), F32),
+            pltpu.VMEM((NZC, 2 * TP), F32),
+            pltpu.VMEM((NZC, NZC, 2 * TP), F32),
             pltpu.VMEM((NZC, 1, TP), F32),
-            pltpu.VMEM((NYX, NZC, 1, TP), F32),
-            dma((NB,)), dma, dma,
+            pltpu.VMEM((NZC, TP), F32),
+            pltpu.VMEM((NYX, NZC, TP), F32),
+            dma((8,)), dma((NB,)), dma, dma,
             dma((2, NB)), dma((2, NB)), dma((2, NB)), dma((2, NB)),
             dma((2, 2)), dma((2, 2)),
-            dma((NYX,)), dma((NYX,)), dma((NZC,)), dma((NZC,)),
+            dma((NZC,)), dma((NZC,)), dma((NYX,)), dma((NYX,)),
             dma((NZC,)), dma((NZC,)), dma((NYX,)), dma((NYX,)),
         ],
         compiler_params=pltpu.CompilerParams(
-            collective_id=0, has_side_effects=True, vmem_limit_bytes=40 << 20
+            collective_id=0, has_side_effects=True, vmem_limit_bytes=54 << 20
         ),
     )(
         state,
@@ -516,13 +594,24 @@
         phase_density.reshape(CH, TP),
         flux_matrices,
         wave_speed,
-        block_tile.reshape(CR, 1),
+        block_tile.reshape(1, CR),
         tile_of_device.reshape(1, DEVICES),
         injection,
         drift_courant.reshape(1, CH),
         energy_weight.reshape(1, CH),
         jnp.asarray(constants()),
     )
+    coupled, drifted = pl.pallas_call(
+        finish,
+        out_shape=(
+            jax.ShapeDtypeStruct((NF, CR, CL, CZ), F32),
+            jax.ShapeDtypeStruct((CH, TP), F32),
+        ),
+        in_specs=[vmem, vmem],
+        out_specs=(hbm, hbm),
+        scratch_shapes=[dma((NF + 1,))],
+        compiler_params=pltpu.CompilerParams(vmem_limit_bytes=1 << 20),
+    )(coupled, drifted)
     return coupled, drifted[None]
 
 

time: 61.4 us -> 47.4 us (0.77)
  local copies, waits for them, and re-layouts: 11.9 us -> 0 us
  Pallas kernels: 48.4 us -> 46.6 us
    unnamed x20 -> x0, local copies, waits for them, and re-layouts: 11.1 us -> none
    pallas_call x1 -> x2, Pallas kernels: 48.4 us -> 46.6 us  [the longest x1 43.3 us: per_device(): pl.pallas_call(kernel, out_shape=(pltpu.VMEM((NF, CR, CL, CZ), F32), pltp...]
    reshape x1 -> x0, local copies, waits for them, and re-layouts: 0.75 us -> none  [per_device(): block_tile.reshape(CR, 1)]
where the time goes in v1:
time: 47.4 us; the launch traced here: 47.3 us
  Pallas kernels  46.6 us (98%)
  between operations  0.64 us (1%)
    pallas_call x1, Pallas kernels, per_device(): pl.pallas_call(kernel, out_shape=(pltpu.VMEM((NF, CR, CL, CZ), F32), pltp...  43.3 us
    pallas_call x1, Pallas kernels, per_device(): pl.pallas_call(finish, out_shape=(jax.ShapeDtypeStruct((NF, CR, CL, CZ),...  3.38 us

profile of v1, /device:TPU:1, one launch (start us, length us, event | category | flops | bytes accessed | tf_op | source)
XLA Modules:
  0.0 47.3 jit_solution(15689962349752531747)
XLA Ops:
  0.6 43.3 %shard_map.122 = (f32[8,64,16,256]{3,2,1,0:T(8,128)S(1)}, f32[200,128]{1,0:T(8,128)S(1)}) custom-call(f32[8,64,16,256]{3,2,1,0:T(8,128)} %state.1, f32[64,16,256]{2,1,0:T(8,128)} %volume.1, f32[200,128]{1,0:T(8,128)} %bitcast.6, f32[2,8,8]{2,1,0:T(8,128)} %matrices_in.1, f32[2]{0:T(128)} %speeds_in.1, s32[1,64]{1,0:T(1,128)} %bitcast.9, s32[1,128]{1,0:T(1,128)} %bitcast.10, ...), custom_call_target="tpu_custom_call" | custom-call | tf_op jit(solution)/shard_map/pallas_call | solution.py:544
  43.9 3.4 %shard_map.123 = (f32[8,64,16,256]{3,2,1,0:T(8,128)}, f32[200,128]{1,0:T(8,128)}) custom-call(f32[8,64,16,256]{3,2,1,0:T(8,128)S(1)} %get-tuple-element.6.fields, f32[200,128]{1,0:T(8,128)S(1)} %get-tuple-element.7.density), custom_call_target="tpu_custom_call" | custom-call | tf_op jit(solution)/shard_map/pallas_call | solution.py:604

commit v2 on v1

v2 whole, which is shorter than its diff:
```python
import numpy as np

import jax
import jax.numpy as jnp
import ml_dtypes
from jax import lax
from jax.experimental import pallas as pl
from jax.experimental.pallas import tpu as pltpu
from jax.sharding import PartitionSpec as P

F32 = jnp.float32
BF16 = jnp.bfloat16
HIGHEST = lax.Precision.HIGHEST
MESH = pl.DeviceIdType.MESH

NF, CR, CL, CZ = 8, 64, 16, 256
ZSEG = 8
DRIFT = 3
CH, TP = 200, 128
NRAD, NLON = 4, 32
NYX, NZC = 16, 8
DEVICES = NRAD * NLON

SCALE = 0.4 * 0.5 / 30.0
ORDER = (0, 7, 1, 2, 3, 4, 5, 6)
ODD = {-3: -1.0, -2: 9.0, -1: -45.0, 1: 45.0, 2: -9.0, 3: 1.0}
EVEN = {-3: 1.0, -2: -6.0, -1: 15.0, 0: -20.0, 1: 15.0, 2: -6.0, 3: 1.0}

RB = 8
NB = CR // RB
SENDS = (0, 2, 4, 6, NB)
PASS = (10,)
LATE = (4, 7)

C_FIX07, C_FIX, C_SEG, C_MASK, C_ODD, C_EVEN, C_EODD, C_EEVEN, C_END = (
    0, 128, 512, 768, 784, 800, 816, 864, 912
)
L_07, H_07, H_EDGE, L_EDGE, L_16, H_16, M_END = 0, 32, 64, 112, 160, 256, 352


def constants():
    t = np.zeros((C_END, 128), np.float32)
    half = 64
    for c in range(2):
        for r in range(4):
            for l in range(CL):
                row = C_FIX07 + (c * 4 + r) * CL + l
                for h in range(2):
                    if l < 3:
                        t[row, h * half + r * 6 + 3 * c + l] = 1
                    if l >= CL - 3:
                        t[row, h * half + 24 + r * 6 + 3 * c + l - (CL - 3)] = 1
    for r in range(4):
        for pos in range(2, NF):
            for l in range(CL):
                row = C_FIX + r * 96 + (pos - 2) * CL + l
                side = 0 if l < 3 else 1
                k = l if l < 3 else l - (CL - 3)
                if 0 <= k < 3:
                    q = 3 * pos + k
                    at = side * 16 + q - 8 if q >= 8 else 32 + side * 8 + r * 2 + q - 6
                    for h in range(2):
                        t[row, h * half + at] = 1
    for z in range(CZ):
        for p in range(TP):
            t[C_SEG + z, p] = z // (CZ // ZSEG) == p % ZSEG
    for l in range(CL):
        for p in range(TP):
            t[C_MASK + l, p] = p // ZSEG == l
    for l in range(CL):
        for f in range(NF):
            for j in range(CL):
                t[C_ODD + l, f * CL + j] = ODD.get(j - l, 0.0)
                t[C_EVEN + l, f * CL + j] = EVEN.get(j - l, 0.0)
    for side in range(2):
        for pos in range(NF):
            for k in range(3):
                row = side * 24 + 3 * pos + k
                for f in range(NF):
                    for j in range(CL):
                        off = j - CL - k if side == 0 else 3 + j - k
                        t[C_EODD + row, f * CL + j] = ODD.get(off, 0.0)
                        if f == ORDER[pos]:
                            t[C_EEVEN + row, f * CL + j] = EVEN.get(off, 0.0)
    return t.astype(ml_dtypes.bfloat16)


def split(x):
    hi = x.astype(BF16)
    return hi, (x - hi.astype(F32)).astype(BF16)


def kernel(
    state, volume, phase, matrices_in, speeds_in, targets_in, tiles_in, injection, courant, weight,
    table_in,
    out, drifted,
    matrices, speeds, targets, tiles, table, inj, cou, wei, cells, vol, dens, lhs, tt1, tt2,
    send0, send1, recv0, recv1, rad_send, rad_recv, cols, pay, hit_db, hit_bd, seg_t, buf, ra,
    part, rb, g0, g2,
    small_sem, load_sem, vol_sem, dens_sem, lon_s0, lon_r0, lon_s1, lon_r1, rad_s, rad_r,
    ra_s, ra_r, rb_s, rb_r, g2_s, g2_r,
):
    rad, lon = lax.axis_index("rad"), lax.axis_index("lon")
    right, left = lax.rem(lon + 1, NLON), lax.rem(lon + NLON - 1, NLON)
    me_yx = rad * (NYX // NRAD) + lax.div(lon, NZC)
    me_zc = lax.rem(lon, NZC)

    def yx_peer(k):
        a = lax.rem(me_yx + k, NYX)
        return a, (lax.div(a, NYX // NRAD), lax.rem(a, NYX // NRAD) * NZC + me_zc)

    def zc_peer(k):
        i = lax.rem(me_zc + k, NZC)
        return i, (rad, lon - me_zc + i)

    small = [
        pltpu.make_async_copy(src, dst, small_sem.at[i])
        for i, (src, dst) in enumerate((
            (matrices_in, matrices), (speeds_in, speeds), (table_in, table),
            (targets_in, targets), (tiles_in, tiles),
            (injection, inj), (courant, cou), (weight, wei),
        ))
    ]
    for copy in small:
        copy.start()

    def load(b):
        return pltpu.make_async_copy(
            state.at[:, pl.ds(b * RB, RB)], cells.at[:, pl.ds(3 + b * RB, RB)], load_sem.at[b]
        )

    for b in [0, 1, NB - 1] + list(range(2, NB - 1)):
        load(b).start()
    vol_copy = pltpu.make_async_copy(volume, vol, vol_sem)
    vol_copy.start()
    dens_copy = pltpu.make_async_copy(phase, dens, dens_sem)
    dens_copy.start()

    barrier = pltpu.get_barrier_semaphore()

    def greet(device):
        pl.semaphore_signal(barrier, inc=1, device_id=device, device_id_type=MESH)

    greet((rad, right))
    greet((rad, left))
    for k in range(1, NYX):
        greet(yx_peer(k)[1])
    for k in range(1, NZC):
        greet(zc_peer(k)[1])

    cells[:, 0:3] = jnp.zeros((NF, 3, CL, CZ), F32)
    cells[:, 3 + CR :] = jnp.zeros((NF, 3, CL, CZ), F32)

    for copy in small:
        copy.wait()
    lane = lax.broadcasted_iota(jnp.int32, (CL, 128), 1)
    sub = lax.broadcasted_iota(jnp.int32, (CL, 128), 0)
    block = lax.shift_right_logical(lane, 4)
    same_l = jnp.bitwise_and(lane, CL - 1) == sub
    odd, even = table[C_ODD : C_ODD + CL].astype(F32), table[C_EVEN : C_EVEN + CL].astype(F32)
    rows_l = []
    for f in range(NF):
        row_r = jnp.zeros((CL, 128), F32)
        row_l = jnp.zeros((CL, 128), F32)
        for g in range(NF):
            row_r = jnp.where(block == g, matrices[0, f, g], row_r)
            row_l = jnp.where(block == g, matrices[1, f, g], row_l)
        rows_l.append(row_l)
        eye = lane == sub + f * CL
        w = (
            (SCALE * speeds[1]) * jnp.where(block == f, even, 0.0)
            - SCALE * row_l * odd
            + jnp.where(eye, 1.0 - 20.0 * SCALE * speeds[0], 0.0)
        )
        whi, wlo = split(w)
        rhi, rlo = split(jnp.where(same_l, (-45.0 * SCALE) * row_r, 0.0))
        if f in (0, 7):
            lo_at, hi_at = L_07 + (0 if f == 0 else CL), H_07 + (0 if f == 0 else CL)
        else:
            lo_at, hi_at = L_16 + (f - 1) * CL, H_16 + (f - 1) * CL
        lhs[lo_at : lo_at + CL, 0:128] = wlo
        lhs[lo_at : lo_at + CL, 128:256] = rlo
        lhs[hi_at : hi_at + CL, 0:128] = whi
        lhs[hi_at : hi_at + CL, 128:256] = rhi
    q = lax.broadcasted_iota(jnp.int32, (24, 128), 0)
    row_e = jnp.zeros((24, 128), F32)
    for pos, f in enumerate(ORDER):
        wide = jnp.concatenate([rows_l[f][0:8]] * 3, axis=0)
        row_e = jnp.where((q >= 3 * pos) & (q < 3 * pos + 3), wide, row_e)
    row_e = jnp.concatenate([row_e, row_e], axis=0)
    we = (SCALE * speeds[1]) * table[C_EEVEN : C_EEVEN + 48].astype(F32) - (
        SCALE * row_e * table[C_EODD : C_EODD + 48].astype(F32)
    )
    ehi, elo = split(we)
    lhs[H_EDGE : H_EDGE + 48, 0:128] = ehi
    lhs[L_EDGE : L_EDGE + 48, 0:128] = elo
    lhs[H_EDGE : H_EDGE + 96, 128:256] = jnp.zeros((96, 128), BF16)

    def row(i):
        return cells[:, i].reshape(NF * CL, CZ)

    def rad_edge(side):
        high = jnp.concatenate([lhs[H_07 : H_07 + 32, 128:], lhs[H_16 : H_16 + 96, 128:]], axis=0)
        low = jnp.concatenate([lhs[L_07 : L_07 + 32, 128:], lhs[L_16 : L_16 + 96, 128:]], axis=0)
        for k in range(3):
            d = jnp.zeros((128, CZ), F32)
            e = jnp.zeros((128, CZ), F32)
            for j in range(3):
                off = j - k - 3 if side == 0 else 3 + j - k
                if off in ODD:
                    u = row(CR + j if side == 0 else 3 + j)
                    d = d + (ODD[off] / 45.0) * u
                    e = e + EVEN[off] * u
            dh, dl = split(d)
            y = (
                jnp.dot(high, dh, preferred_element_type=F32)
                + jnp.dot(low, dh, preferred_element_type=F32)
                + jnp.dot(high, dl, preferred_element_type=F32)
            )
            for pos, f in enumerate(ORDER):
                rad_send[side, pos, k] = y[pos * CL : (pos + 1) * CL] + (
                    SCALE * speeds[0]
                ) * e[f * CL : (f + 1) * CL]

    rad_parts = ((0, 2), (2, 3), (5, 3))

    def rad_copy(side, part_of):
        fields = pl.ds(*rad_parts[part_of])
        return pltpu.make_async_remote_copy(
            src_ref=rad_send.at[side, fields],
            dst_ref=rad_recv.at[side, fields],
            send_sem=rad_s.at[side, part_of],
            recv_sem=rad_r.at[side, part_of],
            device_id=(rad + 1 if side == 0 else rad - 1, lon),
            device_id_type=MESH,
        )

    def send_rad(part_of):
        for side in range(2):
            @pl.when(has[side])
            def _():
                rad_copy(side, part_of).start()

    has = (rad < NRAD - 1, rad > 0)

    def lon_copy(side, part, b):
        src, dst = (send0, recv0) if part == 0 else (send1, recv1)
        ss, rs = (lon_s0, lon_r0) if part == 0 else (lon_s1, lon_r1)
        rows = pl.ds(b * (RB // 4), RB // 4)
        return pltpu.make_async_remote_copy(
            src_ref=src.at[side, rows],
            dst_ref=dst.at[side, rows],
            send_sem=ss.at[side, b],
            recv_sem=rs.at[side, b],
            device_id=(rad, right if side == 0 else left),
            device_id_type=MESH,
        )

    first_eight = lax.broadcasted_iota(jnp.int32, (8, CZ), 0)

    def pick(n, a, b):
        return jnp.where(first_eight < n, a, b)

    def first_pass(g, _):
        tops = ([], [])
        for i in range(4):
            r = 4 * g + i
            m3, m2, m1, u, p1, p2, p3 = (row(r + n) for n in range(7))
            d = (p1 - m1) - 0.2 * ((p2 - m2) - (1.0 / 9.0) * (p3 - m3))
            m3, m2, m1, p1, p2, p3 = (
                jnp.concatenate([x[0:CL], x[112:128]], axis=0) for x in (m3, m2, m1, p1, p2, p3)
            )
            e = (p1 + m1) - 0.4 * ((p2 + m2) - (1.0 / 6.0) * (p3 + m3))
            xh, xl = split(u)
            dh, dl = split(d)
            t1 = jnp.concatenate([xh, dh], axis=0)
            t2 = jnp.concatenate([xl, dl], axis=0)
            tt1[r] = t1
            tt2[r] = t2
            y1 = jnp.dot(lhs[L_07:L_16], t1, preferred_element_type=F32)
            y2 = jnp.dot(lhs[H_07:L_EDGE], t2, preferred_element_type=F32)
            new = (y1[0:32] + y1[32:64] + y2[0:32]) + (15.0 * SCALE * speeds[0]) * e
            out[0, r] = new[0:CL]
            out[7, r] = new[CL:]
            edge = y1[64:112] + y1[112:160] + y2[32:80]
            for side in range(2):
                tops[side].append(edge[side * 24 : side * 24 + 8])
                send1[side, g, i * 16 : (i + 1) * 16] = edge[side * 24 + 8 : side * 24 + 24]
        for side in range(2):
            z0, z1, z2, z3 = tops[side]
            a, b, c = pltpu.roll(z1, 6, axis=0), pltpu.roll(z2, 4, axis=0), pltpu.roll(z3, 2, axis=0)
            send0[side, g, 0:8] = pick(6, z0, a)
            send0[side, g, 8:16] = pick(4, a, b)
            send0[side, g, 16:24] = pick(2, b, c)
            a, b, c = pltpu.roll(z0, 2, axis=0), pltpu.roll(z1, 4, axis=0), pltpu.roll(z2, 6, axis=0)
            send1[side, g, 64:72] = pick(2, a, pick(4, b, pick(6, c, z3)))
        return 0

    def bulk_chunk(b):
        lax.fori_loop(0, RB // 4, lambda i, _: first_pass(b * (RB // 4) + i, _), 0)

    def second_pass(g, _):
        for i in range(4):
            r = 4 * g + i
            m3, m2, m1, _, p1, p2, p3 = (cells[1:7, r + n].reshape(96, CZ) for n in range(7))
            e = (p1 + m1) - 0.4 * ((p2 + m2) - (1.0 / 6.0) * (p3 + m3))
            y1 = jnp.dot(lhs[L_16:M_END], tt1[r], preferred_element_type=F32)
            y2 = jnp.dot(lhs[H_16:M_END], tt2[r], preferred_element_type=F32)
            new = (y1[0:96] + y1[96:192] + y2) + (15.0 * SCALE * speeds[0]) * e
            out[1:7, r] = new.reshape(6, CL, CZ)
        return 0

    def send_early(b):
        lon_copy(0, 0, b).start()
        lon_copy(1, 0, b).start()

    def send_late(b, _):
        lon_copy(0, 1, b).start()
        lon_copy(1, 1, b).start()
        return 0

    load(0).wait()
    load(1).wait()
    bulk_chunk(0)
    pl.semaphore_wait(barrier, 2 + NYX - 1 + NZC - 1)
    send_early(0)
    load(NB - 1).wait()
    rad_edge(0)
    rad_edge(1)
    send_rad(0)
    send_rad(1)

    tile_col = jnp.broadcast_to(tiles[...].astype(F32), (DEVICES, DEVICES)).T
    target_row = jnp.broadcast_to(targets[...].astype(F32), (DEVICES, CR))
    hit = (tile_col[:, 0:CR] == target_row).astype(BF16)
    spread = lax.shift_right_logical(
        lax.broadcasted_iota(jnp.int32, (CR, CR * 8), 1), 3
    ) == lax.broadcasted_iota(jnp.int32, (CR, CR * 8), 0)
    hit_db[...] = jnp.dot(
        hit, spread.astype(F32).astype(BF16), preferred_element_type=F32
    ).astype(BF16)
    target_col = jnp.concatenate(
        [target_row, jnp.zeros((DEVICES, DEVICES - CR), F32)], axis=1
    ).T
    hit_bd[...] = (target_col[0:CR] == tiles[...].astype(F32)).astype(F32).astype(BF16)

    seg_t[...] = (
        jnp.bitwise_and(lax.broadcasted_iota(jnp.int32, (2 * TP, CZ), 0), ZSEG - 1)
        == lax.shift_right_logical(lax.broadcasted_iota(jnp.int32, (2 * TP, CZ), 1), 5)
    ).astype(F32).astype(BF16)

    def rest(b, _):
        @pl.when(b < NB - 2)
        def _():
            load(b + 1).wait()

        bulk_chunk(b)
        send_early(b)
        return 0

    lax.fori_loop(1, NB, rest, 0)
    lax.fori_loop(SENDS[0], SENDS[1], send_late, 0)

    def add_rad(part_of):
        for side in range(2):
            @pl.when(has[1 - side])
            def _():
                rad_copy(side, part_of).wait_recv()
                for pos in range(rad_parts[part_of][0], sum(rad_parts[part_of])):
                    for k in range(3):
                        r = k if side == 0 else CR - 3 + k
                        out[ORDER[pos], r] = out[ORDER[pos], r] + rad_recv[side, pos, k]

    add_rad(0)
    vol_copy.wait()
    seg = table[C_SEG : C_SEG + CZ]
    mask = table[C_MASK : C_MASK + CL].astype(F32)

    def early(b, _):
        for i in range(2):
            lon_copy(0, 0, 2 * b + i).wait_recv()
            lon_copy(1, 0, 2 * b + i).wait_recv()
        highs, lows = [], []
        for h in range(4):
            g = b * 4 + h
            got = jnp.concatenate(
                [recv0[0, g], recv0[1, g], jnp.zeros((16, CZ), F32)], axis=0
            )
            add = jnp.dot(
                table[C_FIX07 : C_FIX07 + 128],
                jnp.concatenate(split(got), axis=0),
                preferred_element_type=F32,
            )
            v = vol[pl.ds(4 * g, 4)].reshape(64, CZ)
            for c, f in enumerate((0, 7)):
                new = out[f, pl.ds(4 * g, 4)].reshape(64, CZ) + add[c * 64 : (c + 1) * 64]
                out[f, pl.ds(4 * g, 4)] = new.reshape(4, CL, CZ)
                yh, yl = split(v * new)
                highs.append(yh)
                lows.append(yl)
        t = jnp.dot(jnp.concatenate(highs + lows, axis=0), seg, preferred_element_type=F32)
        t = t[0:512] + t[512:1024]
        for h in range(4):
            for c in range(2):
                at = (h * 2 + c) * 64
                x = t[at : at + 64].reshape(4, CL, TP) * mask[None]
                pay[pl.ds(b * 128 + h * 32, 32), c * TP : (c + 1) * TP] = (
                    x[:, 0:8] + x[:, 8:16]
                ).reshape(32, TP)
        return 0

    lax.fori_loop(0, NB // 2, early, 0)

    pay_hi, pay_lo = split(pay[...])
    buf[...] = (
        jnp.dot(hit_db[...], pay_hi, preferred_element_type=F32)
        + jnp.dot(hit_db[...], pay_lo, preferred_element_type=F32)
    ).reshape(NYX, NZC, 2 * TP)

    def ra_copy(k):
        a, device = yx_peer(k)
        return pltpu.make_async_remote_copy(
            src_ref=buf.at[a], dst_ref=ra.at[k], send_sem=ra_s.at[k], recv_sem=ra_r.at[k],
            device_id=device, device_id_type=MESH,
        )

    def rb_copy(k):
        i, device = zc_peer(k)
        return pltpu.make_async_remote_copy(
            src_ref=part, dst_ref=rb.at[me_zc], send_sem=rb_s.at[k], recv_sem=rb_r.at[k],
            device_id=device, device_id_type=MESH,
        )

    def g2_copy(k):
        a, device = yx_peer(k)
        return pltpu.make_async_remote_copy(
            src_ref=g0, dst_ref=g2.at[me_yx], send_sem=g2_s.at[k], recv_sem=g2_r.at[k],
            device_id=device, device_id_type=MESH,
        )

    def late(b, _):
        lon_copy(0, 1, b).wait_recv()
        lon_copy(1, 1, b).wait_recv()

        def late_row(i, _):
            r = b * RB + i
            got = jnp.concatenate(
                [recv0[0, r], recv1[0, r], recv0[1, r], recv1[1, r], jnp.zeros((16, CZ), F32)],
                axis=0,
            )
            hi, lo = split(got)
            add = jnp.dot(
                table[C_FIX : C_FIX + 96],
                jnp.concatenate([hi, lo], axis=0),
                preferred_element_type=F32,
            )
            out[1:7, r] = out[1:7, r] + add.reshape(6, CL, CZ)
            return 0

        lax.fori_loop(0, RB, late_row, 0, unroll=8)
        return 0

    def late(b, _):
        lon_copy(0, 1, b).wait_recv()
        lon_copy(1, 1, b).wait_recv()
        for h in range(RB // 4):
            g = b * (RB // 4) + h
            tail = [recv1[0, g, 64:72], recv1[1, g, 64:72], jnp.zeros((16, CZ), F32)]
            for i in range(4):
                got = jnp.concatenate(
                    [recv1[side, g, i * 16 : (i + 1) * 16] for side in range(2)] + tail, axis=0
                )
                add = jnp.dot(
                    table[C_FIX + i * 96 : C_FIX + (i + 1) * 96],
                    jnp.concatenate(split(got), axis=0),
                    preferred_element_type=F32,
                )
                r = 4 * g + i
                out[1:7, r] = out[1:7, r] + add.reshape(6, CL, CZ)
        return 0

    for k in range(1, NYX):
        ra_copy(k).start()
    lax.fori_loop(SENDS[1], SENDS[2], send_late, 0)
    send_rad(2)

    lax.fori_loop(0, PASS[0], second_pass, 0)
    cols[...] = jnp.zeros((8, 256), F32)
    cols[0:2, 0:CH] = inj[...]
    cols[2:3, 0:CH] = cou[...]
    cols[3:4, 0:CH] = wei[...]
    columns = cols[...].T
    channel_rate = jnp.broadcast_to(columns[0:CH, 2:3], (CH, TP))
    channel_weight = jnp.broadcast_to(columns[0:CH, 3:4], (CH, TP))

    def drift(density):
        for _ in range(DRIFT):
            density = density - channel_rate * (density - pltpu.roll(density, 1, axis=1))
        return density

    dens_copy.wait()
    bare = jnp.sum(channel_weight * drift(dens[...]), axis=0, keepdims=True)

    rate_row, weight_row = cols[2:3], cols[3:4]
    keep = 1.0 - rate_row
    powers = (
        keep * keep * keep,
        3.0 * keep * keep * rate_row,
        3.0 * keep * rate_row * rate_row,
        rate_row * rate_row * rate_row,
    )
    taps = [
        [
            jnp.sum(0.5 * weight_row * cols[i : i + 1] * power, axis=1, keepdims=True)
            for power in powers
        ]
        for i in range(2)
    ]

    total = buf[me_yx]
    for k in range(1, NYX):
        ra_copy(k).wait_recv()
        total = total + ra[k]
    part[:, 0 : 2 * TP] = total
    part[:, 2 * TP :] = jnp.broadcast_to(bare, (NZC, TP))
    for k in range(1, NZC):
        rb_copy(k).start()
    lax.fori_loop(SENDS[2], SENDS[3], send_late, 0)
    lax.fori_loop(PASS[0], CR // 4, second_pass, 0)
    add_rad(1)
    lax.fori_loop(0, LATE[0], late, 0)
    rb[me_zc] = part[...]
    for k in range(1, NZC):
        rb_copy(k).wait_recv()
    source = rb[0, :, 0 : 2 * TP]
    for j in range(1, NZC):
        source = source + rb[j, :, 0 : 2 * TP]
    tile_row = lax.broadcasted_iota(jnp.int32, (NZC, TP), 0)
    pressure = jnp.zeros((NZC, TP), F32)
    for j in range(NZC):
        pressure = jnp.where(tile_row == j, rb[j, :, 2 * TP :], pressure)
    for i in range(2):
        s = source[:, i * TP : (i + 1) * TP]
        for n in range(4):
            pressure = pressure + taps[i][n] * (pltpu.roll(s, n, axis=1) if n else s)
    g0[...] = pressure
    for k in range(1, NYX):
        g2_copy(k).start()
    lax.fori_loop(SENDS[3], SENDS[4], send_late, 0)
    g2[me_yx] = pressure

    own = lax.broadcasted_iota(jnp.int32, (NZC, 2 * TP), 0) == me_zc
    mine = jnp.sum(jnp.where(own, source, 0.0), axis=0, keepdims=True)
    drifted[...] = drift(
        dens[...]
        + 0.5 * (columns[0:CH, 0:1] * mine[:, 0:TP] + columns[0:CH, 1:2] * mine[:, TP:])
    )
    add_rad(2)
    lax.fori_loop(LATE[0], LATE[1], late, 0)

    for k in range(1, NYX):
        g2_copy(k).wait_recv()
    back_hi, back_lo = split(g2[...].reshape(DEVICES, TP))
    pay[0:CR, 0:TP] = jnp.dot(hit_bd[...], back_hi, preferred_element_type=F32) + jnp.dot(
        hit_bd[...], back_lo, preferred_element_type=F32
    )

    def nudge(b, _):
        got = pay[pl.ds(b * 16, 16), 0:TP]
        wide = jnp.broadcast_to(got[:, None, :], (16, CL, TP)) * mask[None]
        back = jnp.dot(
            jnp.concatenate(split(wide.reshape(16 * CL, TP)), axis=1),
            seg_t[...],
            preferred_element_type=F32,
        )
        old = out[7, pl.ds(b * 16, 16)].reshape(16 * CL, CZ)
        out[7, pl.ds(b * 16, 16)] = (old + 0.5 * (back - old)).reshape(16, CL, CZ)
        return 0

    lax.fori_loop(0, CR // 16, nudge, 0, unroll=2)
    lax.fori_loop(LATE[1], NB, late, 0)

    def sent(b, _):
        for side in range(2):
            for part in range(2):
                lon_copy(side, part, b).wait_send()
        return 0

    lax.fori_loop(0, NB, sent, 0)
    for side in range(2):
        @pl.when(has[side])
        def _():
            for part_of in range(3):
                rad_copy(side, part_of).wait_send()
    for k in range(1, NYX):
        ra_copy(k).wait_send()
        g2_copy(k).wait_send()
    for k in range(1, NZC):
        rb_copy(k).wait_send()


def finish(fields, density, fields_out, density_out, sem):
    copies = [
        pltpu.make_async_copy(fields.at[f], fields_out.at[f], sem.at[f]) for f in range(NF)
    ] + [pltpu.make_async_copy(density, density_out, sem.at[NF])]
    for copy in copies:
        copy.start()
    for copy in copies:
        copy.wait()


def per_device(
    state, flux_matrices, wave_speed, flux_volume, block_tile, tile_of_device,
    phase_density, injection, drift_courant, energy_weight,
):
    hbm = pl.BlockSpec(memory_space=pltpu.HBM)
    vmem = pl.BlockSpec(memory_space=pltpu.VMEM)
    dma = pltpu.SemaphoreType.DMA
    coupled, drifted = pl.pallas_call(
        kernel,
        out_shape=(
            pltpu.VMEM((NF, CR, CL, CZ), F32),
            pltpu.VMEM((CH, TP), F32),
        ),
        in_specs=[hbm] * 11,
        out_specs=(vmem, vmem),
        scratch_shapes=[
            pltpu.SMEM((2, NF, NF), F32),
            pltpu.SMEM((2,), F32),
            pltpu.VMEM((1, CR), jnp.int32),
            pltpu.VMEM((1, DEVICES), jnp.int32),
            pltpu.VMEM((C_END, 128), BF16),
            pltpu.VMEM((2, CH), F32),
            pltpu.VMEM((1, CH), F32),
            pltpu.VMEM((1, CH), F32),
            pltpu.VMEM((NF, CR + 6, CL, CZ), F32),
            pltpu.VMEM((CR, CL, CZ), F32),
            pltpu.VMEM((CH, TP), F32),
            pltpu.VMEM((M_END, 256), BF16),
            pltpu.VMEM((CR, 256, CZ), BF16),
            pltpu.VMEM((CR, 256, CZ), BF16),
            pltpu.VMEM((2, CR // 4, 24, CZ), F32),
            pltpu.VMEM((2, CR // 4, 72, CZ), F32),
            pltpu.VMEM((2, CR // 4, 24, CZ), F32),
            pltpu.VMEM((2, CR // 4, 72, CZ), F32),
            pltpu.VMEM((2, NF, 3, CL, CZ), F32),
            pltpu.VMEM((2, NF, 3, CL, CZ), F32),
            pltpu.VMEM((8, 256), F32),
            pltpu.VMEM((CR * 8, 2 * TP), F32),
            pltpu.VMEM((DEVICES, CR * 8), BF16),
            pltpu.VMEM((CR, DEVICES), BF16),
            pltpu.VMEM((2 * TP, CZ), BF16),
            pltpu.VMEM((NYX, NZC, 2 * TP), F32),
            pltpu.VMEM((NYX, NZC, 2 * TP), F32),
            pltpu.VMEM((NZC, 3 * TP), F32),
            pltpu.VMEM((NZC, NZC, 3 * TP), F32),
            pltpu.VMEM((NZC, TP), F32),
            pltpu.VMEM((NYX, NZC, TP), F32),
            dma((8,)), dma((NB,)), dma, dma,
            dma((2, NB)), dma((2, NB)), dma((2, NB)), dma((2, NB)),
            dma((2, 3)), dma((2, 3)), dma((NYX,)), dma((NYX,)),
            dma((NZC,)), dma((NZC,)), dma((NYX,)), dma((NYX,)),
        ],
        compiler_params=pltpu.CompilerParams(
            collective_id=0, has_side_effects=True, vmem_limit_bytes=54 << 20
        ),
    )(
        state,
        flux_volume,
        phase_density.reshape(CH, TP),
        flux_matrices,
        wave_speed,
        block_tile.reshape(1, CR),
        tile_of_device.reshape(1, DEVICES),
        injection,
        drift_courant.reshape(1, CH),
        energy_weight.reshape(1, CH),
        jnp.asarray(constants()),
    )
    coupled, drifted = pl.pallas_call(
        finish,
        out_shape=(
            jax.ShapeDtypeStruct((NF, CR, CL, CZ), F32),
            jax.ShapeDtypeStruct((CH, TP), F32),
        ),
        in_specs=[vmem, vmem],
        out_specs=(hbm, hbm),
        scratch_shapes=[dma((NF + 1,))],
        compiler_params=pltpu.CompilerParams(vmem_limit_bytes=1 << 20),
    )(coupled, drifted)
    return coupled, drifted[None]


def solution(mesh):
    in_specs = (
        P(None, "rad", "lon", None),
        P(),
        P(),
        P("rad", "lon", None),
        P("lon", "rad", None),
        P(),
        P(("rad", "lon"), None, None),
        P(),
        P(),
        P(),
    )
    out_specs = (P(None, "rad", "lon", None), P(("rad", "lon"), None, None))
    return jax.shard_map(
        per_device, mesh=mesh, in_specs=in_specs, out_specs=out_specs, check_vma=False
    )
```

time: 47.4 us -> 44.5 us (0.939)
  the two profiles are of different devices: /device:TPU:1 before, /device:TPU:16 now
where the time goes in v2:
time: 44.5 us; the launch traced here: 44.4 us
  Pallas kernels  43.7 us (98%)
  between operations  0.64 us (1%)
    pallas_call x1, Pallas kernels, per_device(): pl.pallas_call(kernel, out_shape=(pltpu.VMEM((NF, CR, CL, CZ), F32), pltp...  40.4 us
    pallas_call x1, Pallas kernels, per_device(): pl.pallas_call(finish, out_shape=(jax.ShapeDtypeStruct((NF, CR, CL, CZ),...  3.38 us

profile of v2, /device:TPU:16, one launch (start us, length us, event | category | flops | bytes accessed | tf_op | source)
XLA Modules:
  0.0 44.4 jit_solution(3567972250118857150)
XLA Ops:
  0.6 40.4 %shard_map.122 = (f32[8,64,16,256]{3,2,1,0:T(8,128)S(1)}, f32[200,128]{1,0:T(8,128)S(1)}) custom-call(f32[8,64,16,256]{3,2,1,0:T(8,128)} %state.1, f32[64,16,256]{2,1,0:T(8,128)} %volume.1, f32[200,128]{1,0:T(8,128)} %bitcast.6, f32[2,8,8]{2,1,0:T(8,128)} %matrices_in.1, f32[2]{0:T(128)} %speeds_in.1, s32[1,64]{1,0:T(1,128)} %bitcast.9, s32[1,128]{1,0:T(1,128)} %bitcast.10, ...), custom_call_target="tpu_custom_call" | custom-call | tf_op jit(solution)/shard_map/pallas_call | solution.py:619
  41.0 3.4 %shard_map.123 = (f32[8,64,16,256]{3,2,1,0:T(8,128)}, f32[200,128]{1,0:T(8,128)}) custom-call(f32[8,64,16,256]{3,2,1,0:T(8,128)S(1)} %get-tuple-element.6.fields, f32[200,128]{1,0:T(8,128)S(1)} %get-tuple-element.7.density), custom_call_target="tpu_custom_call" | custom-call | tf_op jit(solution)/shard_map/pallas_call | solution.py:680

commit v3 on v2

--- a/solution.py
+++ b/solution.py
@@ -28,14 +28,16 @@
 
 RB = 8
 NB = CR // RB
-SENDS = (0, 2, 4, 6, NB)
+SENDS = (0, 3, 5, 7, NB)
 PASS = (10,)
 LATE = (4, 7)
 
 C_FIX07, C_FIX, C_SEG, C_MASK, C_ODD, C_EVEN, C_EODD, C_EEVEN, C_END = (
     0, 128, 512, 768, 784, 800, 816, 864, 912
 )
-L_07, H_07, H_EDGE, L_EDGE, L_16, H_16, M_END = 0, 32, 64, 112, 160, 256, 352
+H_07, L_07, H_EDGE, L_EDGE, HR_07, LR_07, H_16, L_16, HR_16, LR_16, M_END = (
+    0, 32, 64, 112, 160, 192, 224, 320, 416, 512, 608
+)
 
 
 def constants():
@@ -105,13 +107,22 @@
     me_yx = rad * (NYX // NRAD) + lax.div(lon, NZC)
     me_zc = lax.rem(lon, NZC)
 
+    x_at, z_at, core_at = lax.div(lon, NZC), lax.rem(lax.div(lon, 2), 4), lax.rem(lon, 2)
+
     def yx_peer(k):
-        a = lax.rem(me_yx + k, NYX)
-        return a, (lax.div(a, NYX // NRAD), lax.rem(a, NYX // NRAD) * NZC + me_zc)
+        y, x = lax.rem(rad + k // 4, NRAD), lax.rem(x_at + k % 4, NYX // NRAD)
+        return y * (NYX // NRAD) + x, (y, x * NZC + me_zc)
 
     def zc_peer(k):
-        i = lax.rem(me_zc + k, NZC)
-        return i, (rad, lon - me_zc + i)
+        core = 1 - core_at if k % 2 else core_at
+        i = lax.rem(z_at + k // 2, 4) * 2 + core
+        return i, (rad, x_at * NZC + i)
+
+    def hops(n):
+        return min(n, 4 - n)
+
+    yx_order = sorted(range(1, NYX), key=lambda k: -hops(k // 4) - hops(k % 4))
+    zc_order = sorted(range(1, NZC), key=lambda k: -2 * hops(k // 2) - k % 2)
 
     small = [
         pltpu.make_async_copy(src, dst, small_sem.at[i])
@@ -143,9 +154,9 @@
 
     greet((rad, right))
     greet((rad, left))
-    for k in range(1, NYX):
+    for k in yx_order:
         greet(yx_peer(k)[1])
-    for k in range(1, NZC):
+    for k in zc_order:
         greet(zc_peer(k)[1])
 
     cells[:, 0:3] = jnp.zeros((NF, 3, CL, CZ), F32)
@@ -159,6 +170,7 @@
     same_l = jnp.bitwise_and(lane, CL - 1) == sub
     odd, even = table[C_ODD : C_ODD + CL].astype(F32), table[C_EVEN : C_EVEN + CL].astype(F32)
     rows_l = []
+    zero = jnp.zeros((CL, 128), BF16)
     for f in range(NF):
         row_r = jnp.zeros((CL, 128), F32)
         row_l = jnp.zeros((CL, 128), F32)
@@ -174,14 +186,11 @@
         )
         whi, wlo = split(w)
         rhi, rlo = split(jnp.where(same_l, (-45.0 * SCALE) * row_r, 0.0))
-        if f in (0, 7):
-            lo_at, hi_at = L_07 + (0 if f == 0 else CL), H_07 + (0 if f == 0 else CL)
-        else:
-            lo_at, hi_at = L_16 + (f - 1) * CL, H_16 + (f - 1) * CL
-        lhs[lo_at : lo_at + CL, 0:128] = wlo
-        lhs[lo_at : lo_at + CL, 128:256] = rlo
-        lhs[hi_at : hi_at + CL, 0:128] = whi
-        lhs[hi_at : hi_at + CL, 128:256] = rhi
+        at = {0: 0, 7: CL}.get(f, (f - 1) * CL)
+        h, l, hr, lr = (H_07, L_07, HR_07, LR_07) if f in (0, 7) else (H_16, L_16, HR_16, LR_16)
+        for start, high, low in ((h, whi, None), (l, wlo, zero), (hr, rhi, None), (lr, rlo, zero)):
+            lhs[start + at : start + at + CL, 0:128] = high
+            lhs[start + at : start + at + CL, 128:256] = high if low is None else low
     q = lax.broadcasted_iota(jnp.int32, (24, 128), 0)
     row_e = jnp.zeros((24, 128), F32)
     for pos, f in enumerate(ORDER):
@@ -193,15 +202,17 @@
     )
     ehi, elo = split(we)
     lhs[H_EDGE : H_EDGE + 48, 0:128] = ehi
+    lhs[H_EDGE : H_EDGE + 48, 128:256] = ehi
     lhs[L_EDGE : L_EDGE + 48, 0:128] = elo
-    lhs[H_EDGE : H_EDGE + 96, 128:256] = jnp.zeros((96, 128), BF16)
+    lhs[L_EDGE : L_EDGE + 48, 128:256] = jnp.zeros((48, 128), BF16)
 
     def row(i):
         return cells[:, i].reshape(NF * CL, CZ)
 
     def rad_edge(side):
-        high = jnp.concatenate([lhs[H_07 : H_07 + 32, 128:], lhs[H_16 : H_16 + 96, 128:]], axis=0)
-        low = jnp.concatenate([lhs[L_07 : L_07 + 32, 128:], lhs[L_16 : L_16 + 96, 128:]], axis=0)
+        radial = jnp.concatenate(
+            [lhs[HR_07:LR_07], lhs[HR_16:LR_16], lhs[LR_07:H_16], lhs[LR_16:M_END]], axis=0
+        )
         for k in range(3):
             d = jnp.zeros((128, CZ), F32)
             e = jnp.zeros((128, CZ), F32)
@@ -211,12 +222,10 @@
                     u = row(CR + j if side == 0 else 3 + j)
                     d = d + (ODD[off] / 45.0) * u
                     e = e + EVEN[off] * u
-            dh, dl = split(d)
-            y = (
-                jnp.dot(high, dh, preferred_element_type=F32)
-                + jnp.dot(low, dh, preferred_element_type=F32)
-                + jnp.dot(high, dl, preferred_element_type=F32)
+            y = jnp.dot(
+                radial, jnp.concatenate(split(d), axis=0), preferred_element_type=F32
             )
+            y = y[0:128] + y[128:256]
             for pos, f in enumerate(ORDER):
                 rad_send[side, pos, k] = y[pos * CL : (pos + 1) * CL] + (
                     SCALE * speeds[0]
@@ -261,52 +270,65 @@
     def pick(n, a, b):
         return jnp.where(first_eight < n, a, b)
 
-    def first_pass(g, _):
+    def lon_pass(b):
         tops = ([], [])
-        for i in range(4):
-            r = 4 * g + i
-            m3, m2, m1, u, p1, p2, p3 = (row(r + n) for n in range(7))
+        for i in range(RB):
+            r = b * RB + i
+            t1 = jnp.concatenate(split(row(r + 3)), axis=0)
+            tt1[r] = t1
+            y = jnp.dot(lhs[H_07:HR_07], t1, preferred_element_type=F32)
+            new = y[0:32] + y[32:64]
+            out[0, r] = new[0:CL]
+            out[7, r] = new[CL:]
+            edge = y[64:112] + y[112:160]
+            g, j = b * (RB // 4) + i // 4, i % 4
+            for side in range(2):
+                tops[side].append(edge[side * 24 : side * 24 + 8])
+                send1[side, g, j * 16 : (j + 1) * 16] = edge[side * 24 + 8 : side * 24 + 24]
+        for h in range(RB // 4):
+            g = b * (RB // 4) + h
+            for side in range(2):
+                z0, z1, z2, z3 = tops[side][4 * h : 4 * h + 4]
+                a, b1, c = (
+                    pltpu.roll(z1, 6, axis=0), pltpu.roll(z2, 4, axis=0), pltpu.roll(z3, 2, axis=0)
+                )
+                send0[side, g, 0:8] = pick(6, z0, a)
+                send0[side, g, 8:16] = pick(4, a, b1)
+                send0[side, g, 16:24] = pick(2, b1, c)
+                a, b1, c = (
+                    pltpu.roll(z0, 2, axis=0), pltpu.roll(z1, 4, axis=0), pltpu.roll(z2, 6, axis=0)
+                )
+                send1[side, g, 64:72] = pick(2, a, pick(4, b1, pick(6, c, z3)))
+
+    def rad_pass(b, _):
+        for i in range(RB):
+            r = b * RB + i
+            m3, m2, m1, p1, p2, p3 = (row(r + n) for n in (0, 1, 2, 4, 5, 6))
             d = (p1 - m1) - 0.2 * ((p2 - m2) - (1.0 / 9.0) * (p3 - m3))
             m3, m2, m1, p1, p2, p3 = (
                 jnp.concatenate([x[0:CL], x[112:128]], axis=0) for x in (m3, m2, m1, p1, p2, p3)
             )
             e = (p1 + m1) - 0.4 * ((p2 + m2) - (1.0 / 6.0) * (p3 + m3))
-            xh, xl = split(u)
-            dh, dl = split(d)
-            t1 = jnp.concatenate([xh, dh], axis=0)
-            t2 = jnp.concatenate([xl, dl], axis=0)
-            tt1[r] = t1
+            t2 = jnp.concatenate(split(d), axis=0)
             tt2[r] = t2
-            y1 = jnp.dot(lhs[L_07:L_16], t1, preferred_element_type=F32)
-            y2 = jnp.dot(lhs[H_07:L_EDGE], t2, preferred_element_type=F32)
-            new = (y1[0:32] + y1[32:64] + y2[0:32]) + (15.0 * SCALE * speeds[0]) * e
-            out[0, r] = new[0:CL]
-            out[7, r] = new[CL:]
-            edge = y1[64:112] + y1[112:160] + y2[32:80]
-            for side in range(2):
-                tops[side].append(edge[side * 24 : side * 24 + 8])
-                send1[side, g, i * 16 : (i + 1) * 16] = edge[side * 24 + 8 : side * 24 + 24]
-        for side in range(2):
-            z0, z1, z2, z3 = tops[side]
-            a, b, c = pltpu.roll(z1, 6, axis=0), pltpu.roll(z2, 4, axis=0), pltpu.roll(z3, 2, axis=0)
-            send0[side, g, 0:8] = pick(6, z0, a)
-            send0[side, g, 8:16] = pick(4, a, b)
-            send0[side, g, 16:24] = pick(2, b, c)
-            a, b, c = pltpu.roll(z0, 2, axis=0), pltpu.roll(z1, 4, axis=0), pltpu.roll(z2, 6, axis=0)
-            send1[side, g, 64:72] = pick(2, a, pick(4, b, pick(6, c, z3)))
-        return 0
-
-    def bulk_chunk(b):
-        lax.fori_loop(0, RB // 4, lambda i, _: first_pass(b * (RB // 4) + i, _), 0)
+            y = jnp.dot(lhs[HR_07:H_16], t2, preferred_element_type=F32)
+            new = (y[0:32] + y[32:64]) + (15.0 * SCALE * speeds[0]) * e
+            out[0, r] = out[0, r] + new[0:CL]
+            out[7, r] = out[7, r] + new[CL:]
+        return 0
 
     def second_pass(g, _):
         for i in range(4):
             r = 4 * g + i
-            m3, m2, m1, _, p1, p2, p3 = (cells[1:7, r + n].reshape(96, CZ) for n in range(7))
+            m3, m2, m1, p1, p2, p3 = (
+                cells[1:7, r + n].reshape(96, CZ) for n in (0, 1, 2, 4, 5, 6)
+            )
             e = (p1 + m1) - 0.4 * ((p2 + m2) - (1.0 / 6.0) * (p3 + m3))
-            y1 = jnp.dot(lhs[L_16:M_END], tt1[r], preferred_element_type=F32)
-            y2 = jnp.dot(lhs[H_16:M_END], tt2[r], preferred_element_type=F32)
-            new = (y1[0:96] + y1[96:192] + y2) + (15.0 * SCALE * speeds[0]) * e
+            y1 = jnp.dot(lhs[H_16:HR_16], tt1[r], preferred_element_type=F32)
+            y2 = jnp.dot(lhs[HR_16:M_END], tt2[r], preferred_element_type=F32)
+            new = (y1[0:96] + y1[96:192] + y2[0:96] + y2[96:192]) + (
+                15.0 * SCALE * speeds[0]
+            ) * e
             out[1:7, r] = new.reshape(6, CL, CZ)
         return 0
 
@@ -320,16 +342,29 @@
         return 0
 
     load(0).wait()
-    load(1).wait()
-    bulk_chunk(0)
+    lon_pass(0)
     pl.semaphore_wait(barrier, 2 + NYX - 1 + NZC - 1)
     send_early(0)
+    load(1).wait()
+    lon_pass(1)
+    send_early(1)
     load(NB - 1).wait()
     rad_edge(0)
     rad_edge(1)
     send_rad(0)
     send_rad(1)
 
+    def rest(b, _):
+        @pl.when(b < NB - 1)
+        def _():
+            load(b).wait()
+
+        lon_pass(b)
+        send_early(b)
+        return 0
+
+    lax.fori_loop(2, NB, rest, 0)
+    lax.fori_loop(SENDS[0], SENDS[1], send_late, 0)
     tile_col = jnp.broadcast_to(tiles[...].astype(F32), (DEVICES, DEVICES)).T
     target_row = jnp.broadcast_to(targets[...].astype(F32), (DEVICES, CR))
     hit = (tile_col[:, 0:CR] == target_row).astype(BF16)
@@ -349,17 +384,7 @@
         == lax.shift_right_logical(lax.broadcasted_iota(jnp.int32, (2 * TP, CZ), 1), 5)
     ).astype(F32).astype(BF16)
 
-    def rest(b, _):
-        @pl.when(b < NB - 2)
-        def _():
-            load(b + 1).wait()
-
-        bulk_chunk(b)
-        send_early(b)
-        return 0
-
-    lax.fori_loop(1, NB, rest, 0)
-    lax.fori_loop(SENDS[0], SENDS[1], send_late, 0)
+    lax.fori_loop(0, NB, rad_pass, 0)
 
     def add_rad(part_of):
         for side in range(2):
@@ -479,7 +504,7 @@
                 out[1:7, r] = out[1:7, r] + add.reshape(6, CL, CZ)
         return 0
 
-    for k in range(1, NYX):
+    for k in yx_order:
         ra_copy(k).start()
     lax.fori_loop(SENDS[1], SENDS[2], send_late, 0)
     send_rad(2)
@@ -523,7 +548,7 @@
         total = total + ra[k]
     part[:, 0 : 2 * TP] = total
     part[:, 2 * TP :] = jnp.broadcast_to(bare, (NZC, TP))
-    for k in range(1, NZC):
+    for k in zc_order:
         rb_copy(k).start()
     lax.fori_loop(SENDS[2], SENDS[3], send_late, 0)
     lax.fori_loop(PASS[0], CR // 4, second_pass, 0)
@@ -544,7 +569,7 @@
         for n in range(4):
             pressure = pressure + taps[i][n] * (pltpu.roll(s, n, axis=1) if n else s)
     g0[...] = pressure
-    for k in range(1, NYX):
+    for k in yx_order:
         g2_copy(k).start()
     lax.fori_loop(SENDS[3], SENDS[4], send_late, 0)
     g2[me_yx] = pressure

time: 44.5 us -> 42.6 us (0.957)
  the two profiles are of different devices: /device:TPU:16 before, /device:TPU:1 now
where the time goes in v3:
time: 42.6 us; the launch traced here: 42.3 us
  Pallas kernels  41.6 us (98%)
  between operations  0.64 us (2%)
    pallas_call x1, Pallas kernels, per_device(): pl.pallas_call(kernel, out_shape=(pltpu.VMEM((NF, CR, CL, CZ), F32), pltp...  38.2 us
    pallas_call x1, Pallas kernels, per_device(): pl.pallas_call(finish, out_shape=(jax.ShapeDtypeStruct((NF, CR, CL, CZ),...  3.38 us

profile of v3, /device:TPU:1, one launch (start us, length us, event | category | flops | bytes accessed | tf_op | source)
XLA Modules:
  0.0 42.3 jit_solution(12570822316678835062)
XLA Ops:
  0.6 38.2 %shard_map.122 = (f32[8,64,16,256]{3,2,1,0:T(8,128)S(1)}, f32[200,128]{1,0:T(8,128)S(1)}) custom-call(f32[8,64,16,256]{3,2,1,0:T(8,128)} %state.1, f32[64,16,256]{2,1,0:T(8,128)} %volume.1, f32[200,128]{1,0:T(8,128)} %bitcast.6, f32[2,8,8]{2,1,0:T(8,128)} %matrices_in.1, f32[2]{0:T(128)} %speeds_in.1, s32[1,64]{1,0:T(1,128)} %bitcast.9, s32[1,128]{1,0:T(1,128)} %bitcast.10, ...), custom_call_target="tpu_custom_call" | custom-call | tf_op jit(solution)/shard_map/pallas_call | solution.py:644
  38.9 3.4 %shard_map.123 = (f32[8,64,16,256]{3,2,1,0:T(8,128)}, f32[200,128]{1,0:T(8,128)}) custom-call(f32[8,64,16,256]{3,2,1,0:T(8,128)S(1)} %get-tuple-element.6.fields, f32[200,128]{1,0:T(8,128)S(1)} %get-tuple-element.7.density), custom_call_target="tpu_custom_call" | custom-call | tf_op jit(solution)/shard_map/pallas_call | solution.py:705

commit v4 on v3

--- a/solution.py
+++ b/solution.py
@@ -28,7 +28,7 @@
 
 RB = 8
 NB = CR // RB
-SENDS = (0, 3, 5, 7, NB)
+SENDS = (0, 4, 6, 6, NB)
 PASS = (10,)
 LATE = (4, 7)
 

time: 42.6 us -> 40.2 us (0.944)
  Pallas kernels: 41.6 us -> 39.4 us
    pallas_call x1, Pallas kernels: 38.2 us -> 36 us  [per_device(): pl.pallas_call(kernel, out_shape=(pltpu.VMEM((NF, CR, CL, CZ), F32), pltp...]
where the time goes in v4:
time: 40.2 us; the launch traced here: 40 us
  Pallas kernels  39.4 us (98%)
  between operations  0.64 us (2%)
    pallas_call x1, Pallas kernels, per_device(): pl.pallas_call(kernel, out_shape=(pltpu.VMEM((NF, CR, CL, CZ), F32), pltp...  36 us
    pallas_call x1, Pallas kernels, per_device(): pl.pallas_call(finish, out_shape=(jax.ShapeDtypeStruct((NF, CR, CL, CZ),...  3.38 us

profile of v4, /device:TPU:1, one launch (start us, length us, event | category | flops | bytes accessed | tf_op | source)
XLA Modules:
  0.0 40.0 jit_solution(9023642267964758744)
XLA Ops:
  0.6 36.0 %shard_map.122 = (f32[8,64,16,256]{3,2,1,0:T(8,128)S(1)}, f32[200,128]{1,0:T(8,128)S(1)}) custom-call(f32[8,64,16,256]{3,2,1,0:T(8,128)} %state.1, f32[64,16,256]{2,1,0:T(8,128)} %volume.1, f32[200,128]{1,0:T(8,128)} %bitcast.6, f32[2,8,8]{2,1,0:T(8,128)} %matrices_in.1, f32[2]{0:T(128)} %speeds_in.1, s32[1,64]{1,0:T(1,128)} %bitcast.9, s32[1,128]{1,0:T(1,128)} %bitcast.10, ...), custom_call_target="tpu_custom_call" | custom-call | tf_op jit(solution)/shard_map/pallas_call | solution.py:644
  36.7 3.4 %shard_map.123 = (f32[8,64,16,256]{3,2,1,0:T(8,128)}, f32[200,128]{1,0:T(8,128)}) custom-call(f32[8,64,16,256]{3,2,1,0:T(8,128)S(1)} %get-tuple-element.6.fields, f32[200,128]{1,0:T(8,128)S(1)} %get-tuple-element.7.density), custom_call_target="tpu_custom_call" | custom-call | tf_op jit(solution)/shard_map/pallas_call | solution.py:705

commit v5 on v4

--- a/solution.py
+++ b/solution.py
@@ -28,8 +28,9 @@
 
 RB = 8
 NB = CR // RB
-SENDS = (0, 4, 6, 6, NB)
+SENDS = (0, 4, 6, 7, NB)
 PASS = (10,)
+TWO = 0
 LATE = (4, 7)
 
 C_FIX07, C_FIX, C_SEG, C_MASK, C_ODD, C_EVEN, C_EODD, C_EEVEN, C_END = (
@@ -98,9 +99,9 @@
     out, drifted,
     matrices, speeds, targets, tiles, table, inj, cou, wei, cells, vol, dens, lhs, tt1, tt2,
     send0, send1, recv0, recv1, rad_send, rad_recv, cols, pay, hit_db, hit_bd, seg_t, buf, ra,
-    part, rb, g0, g2,
+    part, other, both, rb, g0, g2,
     small_sem, load_sem, vol_sem, dens_sem, lon_s0, lon_r0, lon_s1, lon_r1, rad_s, rad_r,
-    ra_s, ra_r, rb_s, rb_r, g2_s, g2_r,
+    ra_s, ra_r, swap_s, swap_r, rb_s, rb_r, g2_s, g2_r,
 ):
     rad, lon = lax.axis_index("rad"), lax.axis_index("lon")
     right, left = lax.rem(lon + 1, NLON), lax.rem(lon + NLON - 1, NLON)
@@ -449,12 +450,26 @@
             device_id=device, device_id_type=MESH,
         )
 
-    def rb_copy(k):
-        i, device = zc_peer(k)
+    def swap_copy():
         return pltpu.make_async_remote_copy(
-            src_ref=part, dst_ref=rb.at[me_zc], send_sem=rb_s.at[k], recv_sem=rb_r.at[k],
-            device_id=device, device_id_type=MESH,
-        )
+            src_ref=part, dst_ref=other, send_sem=swap_s, recv_sem=swap_r,
+            device_id=(rad, lon + 1 - 2 * core_at), device_id_type=MESH,
+        )
+
+    def z_copy(n, core):
+        return pltpu.make_async_remote_copy(
+            src_ref=both, dst_ref=rb.at[z_at], send_sem=rb_s.at[n, core], recv_sem=rb_r.at[n],
+            device_id=(rad, x_at * NZC + lax.rem(z_at + n, 4) * 2 + core), device_id_type=MESH,
+        )
+
+    def each_z(act):
+        for sender in range(2):
+            @pl.when(core_at == sender)
+            def _():
+                for n in (2, 1, 3):
+                    if sender == {1: 0, 2: TWO, 3: 1}[n]:
+                        for core in range(2):
+                            act(z_copy(n, core))
 
     def g2_copy(k):
         a, device = yx_peer(k)
@@ -548,22 +563,28 @@
         total = total + ra[k]
     part[:, 0 : 2 * TP] = total
     part[:, 2 * TP :] = jnp.broadcast_to(bare, (NZC, TP))
-    for k in zc_order:
-        rb_copy(k).start()
+    swap_copy().start()
+    swap_copy().wait_recv()
+    both[:, 0 : 2 * TP] = part[:, 0 : 2 * TP] + other[:, 0 : 2 * TP]
+    first = core_at == 0
+    both[:, 2 * TP : 3 * TP] = jnp.where(first, part[:, 2 * TP :], other[:, 2 * TP :])
+    both[:, 3 * TP :] = jnp.where(first, other[:, 2 * TP :], part[:, 2 * TP :])
+    each_z(lambda copy: copy.start())
     lax.fori_loop(SENDS[2], SENDS[3], send_late, 0)
     lax.fori_loop(PASS[0], CR // 4, second_pass, 0)
     add_rad(1)
     lax.fori_loop(0, LATE[0], late, 0)
-    rb[me_zc] = part[...]
-    for k in range(1, NZC):
-        rb_copy(k).wait_recv()
+    rb[z_at] = both[...]
+    for n in (1, 2, 3):
+        z_copy(n, 0).wait_recv()
     source = rb[0, :, 0 : 2 * TP]
-    for j in range(1, NZC):
+    for j in range(1, 4):
         source = source + rb[j, :, 0 : 2 * TP]
     tile_row = lax.broadcasted_iota(jnp.int32, (NZC, TP), 0)
     pressure = jnp.zeros((NZC, TP), F32)
     for j in range(NZC):
-        pressure = jnp.where(tile_row == j, rb[j, :, 2 * TP :], pressure)
+        at = (2 + j % 2) * TP
+        pressure = jnp.where(tile_row == j, rb[j // 2, :, at : at + TP], pressure)
     for i in range(2):
         s = source[:, i * TP : (i + 1) * TP]
         for n in range(4):
@@ -620,8 +641,8 @@
     for k in range(1, NYX):
         ra_copy(k).wait_send()
         g2_copy(k).wait_send()
-    for k in range(1, NZC):
-        rb_copy(k).wait_send()
+    swap_copy().wait_send()
+    each_z(lambda copy: copy.wait_send())
 
 
 def finish(fields, density, fields_out, density_out, sem):
@@ -678,13 +699,15 @@
             pltpu.VMEM((NYX, NZC, 2 * TP), F32),
             pltpu.VMEM((NYX, NZC, 2 * TP), F32),
             pltpu.VMEM((NZC, 3 * TP), F32),
-            pltpu.VMEM((NZC, NZC, 3 * TP), F32),
+            pltpu.VMEM((NZC, 3 * TP), F32),
+            pltpu.VMEM((NZC, 4 * TP), F32),
+            pltpu.VMEM((4, NZC, 4 * TP), F32),
             pltpu.VMEM((NZC, TP), F32),
             pltpu.VMEM((NYX, NZC, TP), F32),
             dma((8,)), dma((NB,)), dma, dma,
             dma((2, NB)), dma((2, NB)), dma((2, NB)), dma((2, NB)),
             dma((2, 3)), dma((2, 3)), dma((NYX,)), dma((NYX,)),
-            dma((NZC,)), dma((NZC,)), dma((NYX,)), dma((NYX,)),
+            dma, dma, dma((4, 2)), dma((4,)), dma((NYX,)), dma((NYX,)),
         ],
         compiler_params=pltpu.CompilerParams(
             collective_id=0, has_side_effects=True, vmem_limit_bytes=54 << 20

time: 40.2 us -> 40.6 us (level)
    pallas_call x1, Pallas kernels: 36 us -> 36.4 us  [per_device(): pl.pallas_call(kernel, out_shape=(pltpu.VMEM((NF, CR, CL, CZ), F32), pltp...]
where the time goes in v5:
time: 40.6 us; the launch traced here: 40.5 us
  Pallas kernels  39.8 us (98%)
  between operations  0.64 us (2%)
    pallas_call x1, Pallas kernels, per_device(): pl.pallas_call(kernel, out_shape=(pltpu.VMEM((NF, CR, CL, CZ), F32), pltp...  36.4 us
    pallas_call x1, Pallas kernels, per_device(): pl.pallas_call(finish, out_shape=(jax.ShapeDtypeStruct((NF, CR, CL, CZ),...  3.38 us

profile of v5, /device:TPU:1, one launch (start us, length us, event | category | flops | bytes accessed | tf_op | source)
XLA Modules:
  0.0 40.5 jit_solution(6419147114966223332)
XLA Ops:
  0.6 36.4 %shard_map.122 = (f32[8,64,16,256]{3,2,1,0:T(8,128)S(1)}, f32[200,128]{1,0:T(8,128)S(1)}) custom-call(f32[8,64,16,256]{3,2,1,0:T(8,128)} %state.1, f32[64,16,256]{2,1,0:T(8,128)} %volume.1, f32[200,128]{1,0:T(8,128)} %bitcast.6, f32[2,8,8]{2,1,0:T(8,128)} %matrices_in.1, f32[2]{0:T(128)} %speeds_in.1, s32[1,64]{1,0:T(1,128)} %bitcast.9, s32[1,128]{1,0:T(1,128)} %bitcast.10, ...), custom_call_target="tpu_custom_call" | custom-call | tf_op jit(solution)/shard_map/pallas_call | solution.py:665
  37.1 3.4 %shard_map.123 = (f32[8,64,16,256]{3,2,1,0:T(8,128)}, f32[200,128]{1,0:T(8,128)}) custom-call(f32[8,64,16,256]{3,2,1,0:T(8,128)S(1)} %get-tuple-element.6.fields, f32[200,128]{1,0:T(8,128)S(1)} %get-tuple-element.7.density), custom_call_target="tpu_custom_call" | custom-call | tf_op jit(solution)/shard_map/pallas_call | solution.py:728

commit v6 on v5

--- a/solution.py
+++ b/solution.py
@@ -28,10 +28,10 @@
 
 RB = 8
 NB = CR // RB
-SENDS = (0, 4, 6, 7, NB)
+SENDS = (0, 4, 7, 7, NB)
 PASS = (10,)
 TWO = 0
-LATE = (4, 7)
+LATE = (4, NB)
 
 C_FIX07, C_FIX, C_SEG, C_MASK, C_ODD, C_EVEN, C_EODD, C_EEVEN, C_END = (
     0, 128, 512, 768, 784, 800, 816, 864, 912
@@ -604,28 +604,6 @@
     add_rad(2)
     lax.fori_loop(LATE[0], LATE[1], late, 0)
 
-    for k in range(1, NYX):
-        g2_copy(k).wait_recv()
-    back_hi, back_lo = split(g2[...].reshape(DEVICES, TP))
-    pay[0:CR, 0:TP] = jnp.dot(hit_bd[...], back_hi, preferred_element_type=F32) + jnp.dot(
-        hit_bd[...], back_lo, preferred_element_type=F32
-    )
-
-    def nudge(b, _):
-        got = pay[pl.ds(b * 16, 16), 0:TP]
-        wide = jnp.broadcast_to(got[:, None, :], (16, CL, TP)) * mask[None]
-        back = jnp.dot(
-            jnp.concatenate(split(wide.reshape(16 * CL, TP)), axis=1),
-            seg_t[...],
-            preferred_element_type=F32,
-        )
-        old = out[7, pl.ds(b * 16, 16)].reshape(16 * CL, CZ)
-        out[7, pl.ds(b * 16, 16)] = (old + 0.5 * (back - old)).reshape(16, CL, CZ)
-        return 0
-
-    lax.fori_loop(0, CR // 16, nudge, 0, unroll=2)
-    lax.fori_loop(LATE[1], NB, late, 0)
-
     def sent(b, _):
         for side in range(2):
             for part in range(2):
@@ -640,9 +618,32 @@
                 rad_copy(side, part_of).wait_send()
     for k in range(1, NYX):
         ra_copy(k).wait_send()
-        g2_copy(k).wait_send()
     swap_copy().wait_send()
     each_z(lambda copy: copy.wait_send())
+
+    for k in range(1, NYX):
+        g2_copy(k).wait_recv()
+    back_hi, back_lo = split(g2[...].reshape(DEVICES, TP))
+    pay[0:CR, 0:TP] = jnp.dot(hit_bd[...], back_hi, preferred_element_type=F32) + jnp.dot(
+        hit_bd[...], back_lo, preferred_element_type=F32
+    )
+
+    def nudge(b, _):
+        got = pay[pl.ds(b * 16, 16), 0:TP]
+        wide = jnp.broadcast_to(got[:, None, :], (16, CL, TP)) * mask[None]
+        back = jnp.dot(
+            jnp.concatenate(split(wide.reshape(16 * CL, TP)), axis=1),
+            seg_t[...],
+            preferred_element_type=F32,
+        )
+        old = out[7, pl.ds(b * 16, 16)].reshape(16 * CL, CZ)
+        out[7, pl.ds(b * 16, 16)] = (old + 0.5 * (back - old)).reshape(16, CL, CZ)
+        return 0
+
+    lax.fori_loop(0, CR // 16, nudge, 0, unroll=4)
+
+    for k in range(1, NYX):
+        g2_copy(k).wait_send()
 
 
 def finish(fields, density, fields_out, density_out, sem):

time: 40.6 us -> 40.1 us (0.988); the launches traced: 40.5 us -> 39.4 us
  Pallas kernels: 39.8 us -> 38.8 us
    pallas_call x1, Pallas kernels: 36.4 us -> 35.4 us  [per_device(): pl.pallas_call(kernel, out_shape=(pltpu.VMEM((NF, CR, CL, CZ), F32), pltp...]
where the time goes in v6:
time: 40.1 us; the launch traced here: 39.4 us
  Pallas kernels  38.8 us (97%)
  between operations  0.64 us (2%)
    pallas_call x1, Pallas kernels, per_device(): pl.pallas_call(kernel, out_shape=(pltpu.VMEM((NF, CR, CL, CZ), F32), pltp...  35.4 us
    pallas_call x1, Pallas kernels, per_device(): pl.pallas_call(finish, out_shape=(jax.ShapeDtypeStruct((NF, CR, CL, CZ),...  3.38 us

profile of v6, /device:TPU:1, one launch (start us, length us, event | category | flops | bytes accessed | tf_op | source)
XLA Modules:
  0.0 39.4 jit_solution(15852522020345729047)
XLA Ops:
  0.6 35.4 %shard_map.122 = (f32[8,64,16,256]{3,2,1,0:T(8,128)S(1)}, f32[200,128]{1,0:T(8,128)S(1)}) custom-call(f32[8,64,16,256]{3,2,1,0:T(8,128)} %state.1, f32[64,16,256]{2,1,0:T(8,128)} %volume.1, f32[200,128]{1,0:T(8,128)} %bitcast.6, f32[2,8,8]{2,1,0:T(8,128)} %matrices_in.1, f32[2]{0:T(128)} %speeds_in.1, s32[1,64]{1,0:T(1,128)} %bitcast.9, s32[1,128]{1,0:T(1,128)} %bitcast.10, ...), custom_call_target="tpu_custom_call" | custom-call | tf_op jit(solution)/shard_map/pallas_call | solution.py:666
  36.1 3.4 %shard_map.123 = (f32[8,64,16,256]{3,2,1,0:T(8,128)}, f32[200,128]{1,0:T(8,128)}) custom-call(f32[8,64,16,256]{3,2,1,0:T(8,128)S(1)} %get-tuple-element.6.fields, f32[200,128]{1,0:T(8,128)S(1)} %get-tuple-element.7.density), custom_call_target="tpu_custom_call" | custom-call | tf_op jit(solution)/shard_map/pallas_call | solution.py:729

commit v7 on v6

--- a/solution.py
+++ b/solution.py
@@ -100,7 +100,7 @@
     matrices, speeds, targets, tiles, table, inj, cou, wei, cells, vol, dens, lhs, tt1, tt2,
     send0, send1, recv0, recv1, rad_send, rad_recv, cols, pay, hit_db, hit_bd, seg_t, buf, ra,
     part, other, both, rb, g0, g2,
-    small_sem, load_sem, vol_sem, dens_sem, lon_s0, lon_r0, lon_s1, lon_r1, rad_s, rad_r,
+    lines, small_sem, load_sem, vol_sem, dens_sem, lon_s0, lon_r0, lon_s1, lon_r1, rad_s, rad_r,
     ra_s, ra_r, swap_s, swap_r, rb_s, rb_r, g2_s, g2_r,
 ):
     rad, lon = lax.axis_index("rad"), lax.axis_index("lon")
@@ -155,10 +155,14 @@
 
     greet((rad, right))
     greet((rad, left))
-    for k in yx_order:
+    for k in (2, 1, 3):
+        greet(yx_peer(4 * k)[1])
         greet(yx_peer(k)[1])
-    for k in zc_order:
-        greet(zc_peer(k)[1])
+        greet(zc_peer(2 * k)[1])
+    greet(zc_peer(1)[1])
+
+    def pass_on(device):
+        pl.semaphore_signal(lines, inc=1, device_id=device, device_id_type=MESH)
 
     cells[:, 0:3] = jnp.zeros((NF, 3, CL, CZ), F32)
     cells[:, 3 + CR :] = jnp.zeros((NF, 3, CL, CZ), F32)
@@ -344,8 +348,11 @@
 
     load(0).wait()
     lon_pass(0)
-    pl.semaphore_wait(barrier, 2 + NYX - 1 + NZC - 1)
+    pl.semaphore_wait(barrier, 12)
     send_early(0)
+    for k in (1, 2, 3):
+        pass_on(yx_peer(k)[1])
+    pass_on(zc_peer(1)[1])
     load(1).wait()
     lon_pass(1)
     send_early(1)
@@ -519,6 +526,7 @@
                 out[1:7, r] = out[1:7, r] + add.reshape(6, CL, CZ)
         return 0
 
+    pl.semaphore_wait(lines, 4)
     for k in yx_order:
         ra_copy(k).start()
     lax.fori_loop(SENDS[1], SENDS[2], send_late, 0)
@@ -705,7 +713,7 @@
             pltpu.VMEM((4, NZC, 4 * TP), F32),
             pltpu.VMEM((NZC, TP), F32),
             pltpu.VMEM((NYX, NZC, TP), F32),
-            dma((8,)), dma((NB,)), dma, dma,
+            pltpu.SemaphoreType.REGULAR, dma((8,)), dma((NB,)), dma, dma,
             dma((2, NB)), dma((2, NB)), dma((2, NB)), dma((2, NB)),
             dma((2, 3)), dma((2, 3)), dma((NYX,)), dma((NYX,)),
             dma, dma, dma((4, 2)), dma((4,)), dma((NYX,)), dma((NYX,)),

time: 40.1 us -> 40.1 us (level)
  no operation moved by 1% of the time
where the time goes in v7:
time: 40.1 us; the launch traced here: 39.5 us
  Pallas kernels  38.9 us (97%)
  between operations  0.64 us (2%)
    pallas_call x1, Pallas kernels, per_device(): pl.pallas_call(kernel, out_shape=(pltpu.VMEM((NF, CR, CL, CZ), F32), pltp...  35.5 us
    pallas_call x1, Pallas kernels, per_device(): pl.pallas_call(finish, out_shape=(jax.ShapeDtypeStruct((NF, CR, CL, CZ),...  3.38 us

profile of v7, /device:TPU:1, one launch (start us, length us, event | category | flops | bytes accessed | tf_op | source)
XLA Modules:
  0.0 39.5 jit_solution(1359075136974751745)
XLA Ops:
  0.6 35.5 %shard_map.122 = (f32[8,64,16,256]{3,2,1,0:T(8,128)S(1)}, f32[200,128]{1,0:T(8,128)S(1)}) custom-call(f32[8,64,16,256]{3,2,1,0:T(8,128)} %state.1, f32[64,16,256]{2,1,0:T(8,128)} %volume.1, f32[200,128]{1,0:T(8,128)} %bitcast.6, f32[2,8,8]{2,1,0:T(8,128)} %matrices_in.1, f32[2]{0:T(128)} %speeds_in.1, s32[1,64]{1,0:T(1,128)} %bitcast.9, s32[1,128]{1,0:T(1,128)} %bitcast.10, ...), custom_call_target="tpu_custom_call" | custom-call | tf_op jit(solution)/shard_map/pallas_call | solution.py:674
  36.1 3.4 %shard_map.123 = (f32[8,64,16,256]{3,2,1,0:T(8,128)}, f32[200,128]{1,0:T(8,128)}) custom-call(f32[8,64,16,256]{3,2,1,0:T(8,128)S(1)} %get-tuple-element.6.fields, f32[200,128]{1,0:T(8,128)S(1)} %get-tuple-element.7.density), custom_call_target="tpu_custom_call" | custom-call | tf_op jit(solution)/shard_map/pallas_call | solution.py:737
